TPU v7x, 32 devices: a whole 2x2x4 slice. The times are simulated.
32 devices in a mesh: seq: 2 (over core), batch: 16 (over z, y, x).
Axes of the slice: x: 2, y: 2, z: 4, core: 2. Of those that a mesh axis runs over, the one named last changes fastest.
Arguments:
- tokens: bfloat16 [16, 512, 768], P('batch', 'seq'), may hold values from -6 to 6
- w_qkv: bfloat16 [768, 2304], P('seq'), may hold values from -0.21875 to 0.21875
- q_bias: float32 [768], replicated, may hold values from -3 to 3
- v_bias: float32 [768], replicated, may hold values from -3 to 3
- w_out: bfloat16 [768, 768], P('seq'), may hold values from -1.75 to 1.75
- out_bias: float32 [768], replicated, may hold values from -2 to 2
- attn_gain: float32 [768], replicated, may hold values from 0.1 to 1.9
- attn_shift: float32 [768], replicated, may hold values from -2 to 2
- w_up: bfloat16 [768, 3072], P('seq'), may hold values from -0.21875 to 0.21875
- up_bias: float32 [3072], replicated, may hold values from -3 to 3
- w_down: bfloat16 [3072, 768], P('seq'), may hold values from -0.109375 to 0.109375
- down_bias: float32 [768], replicated, may hold values from -2 to 2
- ffn_gain: float32 [768], replicated, may hold values from 0.1 to 1.9
- ffn_shift: float32 [768], replicated, may hold values from -2 to 2
- seq_len: int32 [16], P('batch'), may hold values from 256 to 512, as said below
- grad_pos: int32 [16, 80], P('batch'), may hold values from 0 to 511, as said below
- grad_count: int32 [16], P('batch'), may hold values from 10 to 80, as said below
- out_grad: bfloat16 [16, 80, 768], P('batch'), may hold values from -6 to 6
Outputs:
- output: bfloat16 [16, 512, 768], P('batch', 'seq')
- grad_tokens: bfloat16 [16, 512, 768], P('batch', 'seq')
- grad_w_qkv: float32 [768, 2304], P('seq')
- grad_q_bias: float32 [768], P('seq')
- grad_v_bias: float32 [768], P('seq')
- grad_w_out: float32 [768, 768], P('seq')
- grad_out_bias: float32 [768], P('seq')
- grad_attn_gain: float32 [768], P('seq')
- grad_attn_shift: float32 [768], P('seq')
- grad_w_up: float32 [768, 3072], P('seq')
- grad_up_bias: float32 [3072], P('seq')
- grad_w_down: float32 [3072, 768], P('seq')
- grad_down_bias: float32 [768], P('seq')
- grad_ffn_gain: float32 [768], P('seq')
- grad_ffn_shift: float32 [768], P('seq')
Inputs may be any that keep to these rules, and one draw needn't show every extreme that they name: `seq_len`: 512 is reached by some sequence in every draw. `grad_count`: 80 is reached by some sequence in every draw. `grad_pos`: the entries of one sequence are distinct and lie below its seq_len; entries at or past grad_count are not used.
All inputs are finite; a program needn't handle non-finite values.
Results may differ from a plain program's by a relative error of at most 0.015.
Values may be sent and summed in bfloat16 or wider, within the bound.
A program may use at most 192 MiB of HBM per device.

v0:
```python
import jax
import jax.numpy as jnp
from jax import lax
from jax.sharding import PartitionSpec as P

HEADS = 12
HEAD_DIM = 64


masked_fill = -1000000000.0
norm_eps = 1e-05


def norm_forward(hidden, gain_vec, offset):
    center = hidden - jnp.mean(hidden, axis=-1, keepdims=True)
    inverse = lax.rsqrt(jnp.mean(center * center, axis=-1, keepdims=True) + norm_eps)
    unit_rows = center * inverse
    return (unit_rows * gain_vec + offset, unit_rows, inverse)


def norm_backward(upstream, unit_rows, inverse, gain_vec):
    scaled = upstream * gain_vec
    inner = (
        scaled
        - jnp.mean(scaled, axis=-1, keepdims=True)
        - unit_rows * jnp.mean(scaled * unit_rows, axis=-1, keepdims=True)
    )
    return (inverse * inner, jnp.sum(upstream * unit_rows, axis=0), jnp.sum(upstream, axis=0))


def exact_gelu(values):
    return jax.nn.gelu(values, approximate=False)


def masked_scores(head_block, key_limit, local_heads, score_scale):
    length = head_block.shape[0]
    queries = head_block[:, 0].reshape(length, local_heads, HEAD_DIM)
    key_rows = head_block[:, 1].reshape(length, local_heads, HEAD_DIM)
    values = head_block[:, 2].reshape(length, local_heads, HEAD_DIM)
    scores = (
        jnp.einsum("qhd,khd->hqk", queries, key_rows, preferred_element_type=jnp.float32)
        * score_scale
    )
    key_valid = jnp.arange(length) < key_limit
    scores = jnp.where(key_valid[None, None, :], scores, masked_fill)
    return (queries, key_rows, values, scores)


def attend_forward(map_entry, local_heads, score_scale):
    head_block, key_limit = map_entry
    length = head_block.shape[0]
    queries, key_rows, values, scores = masked_scores(
        head_block, key_limit, local_heads, score_scale
    )
    peak = jnp.max(scores, axis=-1, keepdims=True)
    exp_scores = jnp.exp(scores - peak)
    row_total = jnp.sum(exp_scores, axis=-1, keepdims=True)
    attn_probs = exp_scores / row_total
    mixed = jnp.einsum(
        "hqk,khd->qhd", attn_probs.astype(jnp.bfloat16), values, preferred_element_type=jnp.float32
    )
    return (
        mixed.reshape(length, local_heads * HEAD_DIM).astype(jnp.bfloat16),
        (peak + jnp.log(row_total))[..., 0],
    )


def attend_backward(map_entry, local_heads, score_scale):
    head_block, log_total, d_context, key_limit = map_entry
    length = head_block.shape[0]
    queries, key_rows, values, scores = masked_scores(
        head_block, key_limit, local_heads, score_scale
    )
    attn_probs = jnp.exp(scores - log_total[..., None])
    d_heads = d_context.reshape(length, local_heads, HEAD_DIM)
    d_probs = jnp.einsum("qhd,khd->hqk", d_heads, values, preferred_element_type=jnp.float32)
    d_values = jnp.einsum(
        "hqk,qhd->khd", attn_probs.astype(jnp.bfloat16), d_heads, preferred_element_type=jnp.float32
    )
    d_scores = attn_probs * (d_probs - jnp.sum(attn_probs * d_probs, axis=-1, keepdims=True))
    d_low = d_scores.astype(jnp.bfloat16)
    d_queries = (
        jnp.einsum("hqk,khd->qhd", d_low, key_rows, preferred_element_type=jnp.float32)
        * score_scale
    )
    d_keys = (
        jnp.einsum("hqk,qhd->khd", d_low, queries, preferred_element_type=jnp.float32) * score_scale
    )
    stacked = jnp.stack([d_queries, d_keys, d_values], axis=1)
    return stacked.reshape(length, 3, local_heads * HEAD_DIM).astype(jnp.bfloat16)


def body(
    tokens,
    w_qkv,
    q_bias,
    v_bias,
    w_out,
    out_bias,
    attn_gain,
    attn_shift,
    w_up,
    up_bias,
    w_down,
    down_bias,
    ffn_gain,
    ffn_shift,
    seq_len,
    grad_pos,
    grad_count,
    out_grad,
):
    seq_local, half_len, model_width = tokens.shape
    shards = lax.axis_size("seq")
    local_heads = HEADS // shards
    score_scale = HEAD_DIM ** (-0.5)
    row_count = seq_local * half_len
    tok_rows = tokens.reshape(row_count, model_width)
    full_qkv, full_out, full_up, full_down = (
        lax.all_gather(w_qkv, "seq", axis=0, tiled=True),
        lax.all_gather(w_out, "seq", axis=0, tiled=True),
        lax.all_gather(w_up, "seq", axis=0, tiled=True),
        lax.all_gather(w_down, "seq", axis=0, tiled=True),
    )
    bias_qkv = jnp.concatenate([q_bias, jnp.zeros_like(q_bias), v_bias])
    packed = (jnp.dot(tok_rows, full_qkv, preferred_element_type=jnp.float32) + bias_qkv).astype(
        jnp.bfloat16
    )
    grouped = lax.all_to_all(
        packed.reshape(seq_local, half_len, 3, model_width),
        "seq",
        split_axis=3,
        concat_axis=1,
        tiled=True,
    )
    context, log_totals = lax.map(
        lambda map_entry: attend_forward(map_entry, local_heads, score_scale), (grouped, seq_len)
    )
    returned = lax.all_to_all(context, "seq", split_axis=1, concat_axis=2, tiled=True)
    ctx_rows = returned.reshape(row_count, model_width)
    attn_out = jnp.dot(ctx_rows, full_out, preferred_element_type=jnp.float32) + out_bias
    normed, unit_one, inverse_one = norm_forward(
        tok_rows.astype(jnp.float32) + attn_out, attn_gain, attn_shift
    )
    normed_low = normed.astype(jnp.bfloat16)
    up_proj = jnp.dot(normed_low, full_up, preferred_element_type=jnp.float32) + up_bias
    active, gelu_pull = jax.vjp(exact_gelu, up_proj)
    active_low = active.astype(jnp.bfloat16)
    lowered = jnp.dot(active_low, full_down, preferred_element_type=jnp.float32) + down_bias
    output, unit_two, inverse_two = norm_forward(normed + lowered, ffn_gain, ffn_shift)
    row_start = lax.axis_index("seq") * half_len
    places = row_start + jnp.arange(half_len, dtype=jnp.int32)
    slot_count = grad_pos.shape[1]
    hit_table = (grad_pos[:, None, :] == places[None, :, None]) & (
        jnp.arange(slot_count)[None, None, :] < grad_count[:, None, None]
    )
    cotangent = jnp.einsum(
        "stj,sjd->std", hit_table.astype(jnp.bfloat16), out_grad, preferred_element_type=jnp.float32
    ).reshape(row_count, model_width)
    d_two, grad_ffn_gain, grad_ffn_shift = norm_backward(cotangent, unit_two, inverse_two, ffn_gain)
    d_down = d_two.astype(jnp.bfloat16)
    grad_down_bias = jnp.sum(d_down.astype(jnp.float32), axis=0)
    grad_w_down = jnp.einsum("nf,nd->fd", active_low, d_down, preferred_element_type=jnp.float32)
    d_active = jnp.einsum("nd,fd->nf", d_down, full_down, preferred_element_type=jnp.float32)
    d_up = gelu_pull(d_active)[0].astype(jnp.bfloat16)
    grad_up_bias = jnp.sum(d_up.astype(jnp.float32), axis=0)
    grad_w_up = jnp.einsum("nd,nf->df", normed_low, d_up, preferred_element_type=jnp.float32)
    d_normed = d_two + jnp.einsum("nf,df->nd", d_up, full_up, preferred_element_type=jnp.float32)
    d_one, grad_attn_gain, grad_attn_shift = norm_backward(
        d_normed, unit_one, inverse_one, attn_gain
    )
    d_attn = d_one.astype(jnp.bfloat16)
    grad_out_bias = jnp.sum(d_attn.astype(jnp.float32), axis=0)
    grad_w_out = jnp.einsum("nc,nd->cd", ctx_rows, d_attn, preferred_element_type=jnp.float32)
    d_context = jnp.einsum(
        "nd,cd->nc", d_attn, full_out, preferred_element_type=jnp.float32
    ).astype(jnp.bfloat16)
    d_grouped = lax.all_to_all(
        d_context.reshape(seq_local, half_len, model_width),
        "seq",
        split_axis=2,
        concat_axis=1,
        tiled=True,
    )
    d_packed = lax.map(
        lambda map_entry: attend_backward(map_entry, local_heads, score_scale),
        (grouped, log_totals, d_grouped, seq_len),
    )
    d_back = lax.all_to_all(d_packed, "seq", split_axis=1, concat_axis=3, tiled=True).reshape(
        row_count, 3 * model_width
    )
    grad_q_bias = jnp.sum(d_back[:, :model_width].astype(jnp.float32), axis=0)
    grad_v_bias = jnp.sum(d_back[:, 2 * model_width :].astype(jnp.float32), axis=0)
    grad_w_qkv = jnp.einsum("nd,ne->de", tok_rows, d_back, preferred_element_type=jnp.float32)
    d_tokens = d_one + jnp.einsum("ne,de->nd", d_back, full_qkv, preferred_element_type=jnp.float32)
    (
        total_w_qkv,
        total_q_bias,
        total_v_bias,
        total_w_out,
        total_out_bias,
        total_attn_gain,
        total_attn_shift,
        total_w_up,
        total_up_bias,
        total_w_down,
        total_down_bias,
        total_ffn_gain,
        total_ffn_shift,
    ) = (
        lax.psum_scatter(
            grad_w_qkv.astype(jnp.bfloat16), "seq", scatter_dimension=0, tiled=True
        ).astype(jnp.float32),
        lax.psum_scatter(
            grad_q_bias.astype(jnp.bfloat16), "seq", scatter_dimension=0, tiled=True
        ).astype(jnp.float32),
        lax.psum_scatter(
            grad_v_bias.astype(jnp.bfloat16), "seq", scatter_dimension=0, tiled=True
        ).astype(jnp.float32),
        lax.psum_scatter(
            grad_w_out.astype(jnp.bfloat16), "seq", scatter_dimension=0, tiled=True
        ).astype(jnp.float32),
        lax.psum_scatter(
            grad_out_bias.astype(jnp.bfloat16), "seq", scatter_dimension=0, tiled=True
        ).astype(jnp.float32),
        lax.psum_scatter(
            grad_attn_gain.astype(jnp.bfloat16), "seq", scatter_dimension=0, tiled=True
        ).astype(jnp.float32),
        lax.psum_scatter(
            grad_attn_shift.astype(jnp.bfloat16), "seq", scatter_dimension=0, tiled=True
        ).astype(jnp.float32),
        lax.psum_scatter(
            grad_w_up.astype(jnp.bfloat16), "seq", scatter_dimension=0, tiled=True
        ).astype(jnp.float32),
        lax.psum_scatter(
            grad_up_bias.astype(jnp.bfloat16), "seq", scatter_dimension=0, tiled=True
        ).astype(jnp.float32),
        lax.psum_scatter(
            grad_w_down.astype(jnp.bfloat16), "seq", scatter_dimension=0, tiled=True
        ).astype(jnp.float32),
        lax.psum_scatter(
            grad_down_bias.astype(jnp.bfloat16), "seq", scatter_dimension=0, tiled=True
        ).astype(jnp.float32),
        lax.psum_scatter(
            grad_ffn_gain.astype(jnp.bfloat16), "seq", scatter_dimension=0, tiled=True
        ).astype(jnp.float32),
        lax.psum_scatter(
            grad_ffn_shift.astype(jnp.bfloat16), "seq", scatter_dimension=0, tiled=True
        ).astype(jnp.float32),
    )
    (
        total_w_qkv,
        total_q_bias,
        total_v_bias,
        total_w_out,
        total_out_bias,
        total_attn_gain,
        total_attn_shift,
        total_w_up,
        total_up_bias,
        total_w_down,
        total_down_bias,
        total_ffn_gain,
        total_ffn_shift,
    ) = lax.psum(
        (
            total_w_qkv,
            total_q_bias,
            total_v_bias,
            total_w_out,
            total_out_bias,
            total_attn_gain,
            total_attn_shift,
            total_w_up,
            total_up_bias,
            total_w_down,
            total_down_bias,
            total_ffn_gain,
            total_ffn_shift,
        ),
        "batch",
    )
    out_block = output.astype(jnp.bfloat16).reshape(seq_local, half_len, model_width)
    grad_block = d_tokens.astype(jnp.bfloat16).reshape(seq_local, half_len, model_width)
    return (
        out_block,
        grad_block,
        total_w_qkv,
        total_q_bias,
        total_v_bias,
        total_w_out,
        total_out_bias,
        total_attn_gain,
        total_attn_shift,
        total_w_up,
        total_up_bias,
        total_w_down,
        total_down_bias,
        total_ffn_gain,
        total_ffn_shift,
    )


def solution(mesh):
    return jax.shard_map(
        body,
        mesh=mesh,
        in_specs=(
            P("batch", "seq", None),
            P("seq", None),
            P(),
            P(),
            P("seq", None),
            P(),
            P(),
            P(),
            P("seq", None),
            P(),
            P("seq", None),
            P(),
            P(),
            P(),
            P("batch"),
            P("batch", None),
            P("batch"),
            P("batch", None, None),
        ),
        out_specs=(
            P("batch", "seq", None),
            P("batch", "seq", None),
            P("seq", None),
            P("seq"),
            P("seq"),
            P("seq", None),
            P("seq"),
            P("seq"),
            P("seq"),
            P("seq", None),
            P("seq"),
            P("seq", None),
            P("seq"),
            P("seq"),
            P("seq"),
        ),
        check_vma=False,
    )
```

profile of v0, /device:TPU:0, one launch (start us, length us, event | category | flops | bytes accessed | tf_op | source)
XLA Modules:
  0.0 811.6 jit_solution(3011633205040058357)
XLA Ops:
  7.3 0.7 all-gather.5.cloned.1.call-update
  8.0 0.7 all-gather.7.cloned.1.call-update
  8.8 0.7 all-gather.9.cloned.1.call-update
  9.5 0.5 all-gather.11.cloned.1.call-update
  11.5 0.3 fusion.29
  11.8 13.2 %all-gather.5.cloned.1.call-done = bf16[768,2304]{1,0:T(8,128)(2,1)} async-done(((bf16[384,2304]{1,0:T(8,128)(2,1)}), bf16[768,2304]{1,0:T(8,128)(2,1)}) %all-gather.5.cloned.1.call-update) | async-done | bytes 3538960 | tf_op jit(solution)/shard_map/all_gather | solution.py:120
  25.0 3.1 fusion.3
  28.2 0.6 copy.85
  28.8 1.0 copy.86
  29.8 5.0 all_to_all.60
  35.0 0.7 copy.88
  36.3 4.1 fusion.47
  40.6 3.8 fusion
  44.4 0.9 copy-done.2
  45.3 1.2 fusion.22
  46.5 1.1 copy.93
  47.7 0.5 broadcast.155
  48.2 3.1 reduce.5
  51.4 4.3 all_to_all.61
  55.7 0.4 reshape.271
  56.4 2.0 fusion.48
  58.7 11.3 %multiply_convert_fusion.1 = (bf16[256,3072]{1,0:T(8,128)(2,1)S(1)}, f32[256,3072]{1,0:T(8,128)}, f32[256,3072]{1,0:T(8,128)}) fusion(f32[3072]{0:T(1024)S(1)} %copy-done.31, bf16[768,3072]{1,0:T(8,128)(2,1)} %all-gather.9.cloned.1.call-done, f32[256,768]{1,0:T(8,128)S(1)} %get-tuple-element.168, f32[768]{0:T(1024)S(1)} %copy-done.24, ...), kind=kOutput, calls=%fused_computation.20 | convolution fusion | flops 1260847104 | bytes 13389824 | tf_op jit(solution)/shard_map/dot_general | solution.py:146
  70.0 1.2 all-gather.11.cloned.1.call-done
  71.3 4.0 fusion.49
  75.6 1.2 multiply_reduce_fusion.1
  76.8 0.3 convert_reduce_fusion.1
  77.1 0.4 copy-done.34
  77.5 2.1 fusion.50
  79.7 1.8 multiply_reduce_fusion.2
  81.5 0.3 convert_reduce_fusion
  81.8 1.5 convolution_convert_fusion.3
  83.3 0.5 fusion.23
  83.9 0.6 copy.95
  84.5 3.1 reduce.6
  87.7 4.0 all_to_all.62
  91.8 0.4 reshape.273
  92.2 0.4 copy.96
  92.9 3.9 fusion.19
  96.8 1.8 copy.102
  98.6 10.0 %reduce-scatter.13.cloned.1.call-start = ((), (), s32[]{:S(2)}) async-start(), calls=%async_computation.15 | async-start | bytes 5308416
  108.7 4.1 multiply_reduce_fusion
  112.8 4.0 multiply_convert_fusion
  116.8 1.8 fusion.18
  118.6 2.9 copy.101
  121.5 2.4 fusion.17
  123.9 2.5 copy.100
  126.4 3.8 pad_maximum_fusion
  130.2 5.0 all_to_all.63
  135.4 0.6 copy.104
  136.2 2.9 fusion.2
  139.1 5.8 copy.110
  145.0 1.1 copy-done.4
  146.0 5.2 convolution_convert_fusion.1
  151.3 1.8 copy-done.9
  153.1 4.8 convolution_convert_fusion
  157.9 0.6 copy-done.33
  158.5 0.6 dynamic-slice
  160.7 3.4 all-reduce.10
  164.8 3.9 fusion.24
  168.7 2.9 copy.111
  171.7 3.0 reduce-scatter.9.cloned.1.call-done
  174.7 16.7 %reduce-scatter.11.cloned.1.call-done = bf16[1536,768]{1,0:T(8,128)(2,1)} async-done(((bf16[3072,768]{1,0:T(8,128)(2,1)}), bf16[1536,768]{1,0:T(8,128)(2,1)}) %reduce-scatter.11.cloned.1.call-update) | async-done | bytes 2359312 | tf_op jit(solution)/shard_map/reduce_scatter | solution.py:238
  191.5 608.0 %all-reduce.12 = (f32[384,2304]{0,1:T(8,128)}, f32[384]{0:T(512)}, f32[384]{0:T(512)}, f32[384,768]{1,0:T(8,128)}, f32[384]{0:T(512)}, /*index=5*/f32[384]{0:T(5...) all-reduce(bf16[384,2304]{0,1:T(8,128)(2,1)S(1)} %copy.111, ...), channel_id=1, replica_groups=mesh['seq'=2,'batch'=16] {'batch'}, use_global_device_ids=true, to_apply=%region_12.13 | all-reduce | flops 3543552 | bytes 21270528 | tf_op jit(solution)/shard_map/psum | solution.py:265
  799.4 5.2 copy.105
  (129 shorter events, 4.0 us)
Async XLA Ops:
  7.2 4.3 copy-start
  7.2 4.2 copy-start.28
  7.2 4.2 copy-start.29
  7.2 4.3 copy-start.30
  7.2 17.8 %all-gather.5.cloned.1.call-start = ((), (), s32[]{:S(2)}) async-start(), calls=%async_computation.8 | async-start | bytes 5308416 | tf_op jit(solution)/shard_map/all_gather | solution.py:120
  8.0 17.1 %copy-start.16 = (bf16[1,256,768]{2,1,0:T(8,128)(2,1)S(1)}, bf16[1,256,768]{2,1,0:T(8,128)(2,1)}, u32[]{:S(2)}) copy-start(bf16[1,256,768]{2,1,0:T(8,128)(2,1)} %param.18) | copy-start | bytes 1179652
  8.0 48.4 %all-gather.7.cloned.1.call-start = ((), (), s32[]{:S(2)}) async-start(), calls=%async_computation.9 | async-start | bytes 1769472 | tf_op jit(solution)/shard_map/all_gather | solution.py:121
  8.7 49.9 %all-gather.9.cloned.1.call-start = ((), (), s32[]{:S(2)}) async-start(), calls=%async_computation.10 | async-start | bytes 7077888 | tf_op jit(solution)/shard_map/all_gather | solution.py:122
  9.5 61.8 %all-gather.11.cloned.1.call-start = ((), (), s32[]{:S(2)}) async-start(), calls=%async_computation.11 | async-start | bytes 7077888 | tf_op jit(solution)/shard_map/all_gather | solution.py:123
  10.0 158.7 %reduce-scatter.7.cloned.1.call-start = ((), (), s32[]{:S(2)}) async-start(), calls=%async_computation.12 | async-start | bytes 1769472 | tf_op jit(solution)/shard_map/reduce_scatter | solution.py:220
  36.0 4.3 copy-start.10
  36.3 4.1 copy-start.11
  40.6 3.9 copy-start.19
  40.6 4.7 copy-start.2
  47.6 8.8 %copy-start.17 = (bf16[1,256,768]{2,1,0:T(8,128)(2,1)S(1)}, bf16[1,256,768]{2,1,0:T(8,128)(2,1)}, u32[]{:S(2)}) copy-start(bf16[1,256,768]{2,1,0:T(8,128)(2,1)} %param.18) | copy-start | bytes 1179652
  47.6 8.7 %copy-start.26 = (f32[768]{0:T(1024)S(1)}, f32[768]{0:T(1024)}, u32[]{:S(2)}) copy-start(f32[768]{0:T(1024)} %param.23) | copy-start | bytes 9220
  55.7 3.0 copy-start.23
  55.7 3.0 copy-start.24
  55.7 3.0 copy-start.31
  56.3 2.3 copy-start.13
  58.4 23.1 %copy-start.3 = (f32[256,768]{1,0:T(8,128)}, f32[256,768]{1,0:T(8,128)S(1)}, u32[]{:S(2)}) copy-start(f32[256,768]{1,0:T(8,128)S(1)} %get-tuple-element.168) | copy-start | bytes 2359300
  58.6 12.6 %copy-start.32 = (f32[768]{0:T(1024)S(1)}, f32[768]{0:T(1024)}, u32[]{:S(2)}) copy-start(f32[768]{0:T(1024)} %param.29) | copy-start | bytes 9220
  70.0 5.3 copy-start.8
  71.2 5.9 slice-start.2
  71.2 4.3 copy-start.25
  71.2 4.3 copy-start.27
  71.3 5.9 slice-start.3
  71.3 5.9 copy-start.35
  75.3 2.2 copy-start.34
  76.8 2.9 slice-start
  77.1 2.6 copy-start.15
  77.5 2.2 slice-start.1
  79.6 1.8 copy-start.21
  79.7 2.1 copy-start.14
  81.5 1.9 copy-start.7
  81.8 5.8 copy-start.5
  92.9 15.8 %copy-start.20 = (bf16[512,1,384]{0,2,1:T(8,128)(2,1)S(1)}, bf16[512,1,384]{0,2,1:T(8,128)(2,1)}, u32[]{:S(2)}) copy-start(bf16[512,1,384]{0,2,1:T(8,128)(2,1)} %copy-done.19) | copy-start | bytes 1179652
  98.6 70.1 %reduce-scatter.13.cloned.1.call-start = ((), (), s32[]{:S(2)}) async-start(), calls=%async_computation.15 | async-start | bytes 5308416
  112.8 4.0 copy-start.12
  135.2 1.0 copy-start.18
  144.9 1.1 copy-start.4
  144.9 29.8 %reduce-scatter.9.cloned.1.call-start = ((), (), s32[]{:S(2)}) async-start(), calls=%async_computation.13 | async-start | bytes 7077888 | tf_op jit(solution)/shard_map/reduce_scatter | solution.py:232
  151.2 1.9 copy-start.9
  151.3 40.2 %reduce-scatter.11.cloned.1.call-start = ((), (), s32[]{:S(2)}) async-start(), calls=%async_computation.14 | async-start | bytes 7077888 | tf_op jit(solution)/shard_map/reduce_scatter | solution.py:238
  157.9 0.7 copy-start.33
  157.9 6.9 copy-start.6
  168.7 22.7 %copy-start.22 = (bf16[384,768]{1,0:T(8,128)(2,1)S(1)}, bf16[384,768]{1,0:T(8,128)(2,1)}, u32[]{:S(2)}) copy-start(bf16[384,768]{1,0:T(8,128)(2,1)} %reduce-scatter.7.cloned.1.call-done) | copy-start | bytes 1769476
  799.4 5.2 copy-start.1
Sparse Core Ops, SparseCore 0:
  9.6 15.4 all-gather.4
  26.6 10.3 all-gather.6
  38.6 15.6 all-gather.8
  55.6 15.6 all-gather.10
  98.8 9.6 reduce-scatter.6
  145.1 12.8 reduce-scatter.12
  160.8 13.8 reduce-scatter.8
  177.6 13.8 reduce-scatter.10
where the time goes:
time: 821 us; the launch traced here: 812 us
  blocking collectives  630 us (77%)
  matrix products  60.9 us (7%)
  waiting for transfers between devices  36.9 us (4%)
  local copies, waits for them, and re-layouts  35 us (4%)
  other arithmetic  21.1 us (3%)
  between operations  17.7 us (2%)
  starting transfers between devices  10.3 us (1%)
    psum x1, blocking collectives, body(): lax.psum((total_w_qkv, total_q_bias, total_v_bias, total_w_out, total_out...  608 us
    unnamed x91, local copies, waits for them, and re-layouts  21.2 us
    reduce_scatter x1, waiting for transfers between devices, body(): lax.psum_scatter(grad_w_down.astype(jnp.bfloat16), 'seq', scatter_dimensi...  16.7 us
  transfers between devices with their start and end apart: 8, of which 4 were waited for; matrix products, arithmetic and copies ran while one was open for 10% of the time, Pallas kernels for 0%

commit v1 on v0

v1 whole, which is shorter than its diff:
```python
import functools
import math

import jax
import jax.numpy as jnp
import numpy as np
from jax import lax
from jax.experimental import pallas as pl
from jax.experimental.pallas import tpu as pltpu
from jax.sharding import PartitionSpec as P

HEAD_DIM = 64
NORM_EPS = 1e-05
MASKED = -1000000000.0
BF = jnp.bfloat16
F32 = jnp.float32
MESH = pl.DeviceIdType.MESH
VMEM_LIMIT = 63 * 1024 * 1024


def mm(a, b):
    return lax.dot_general(a, b, (((1,), (0,)), ((), ())), preferred_element_type=F32)


def mm_nt(a, b):
    return lax.dot_general(a, b, (((1,), (1,)), ((), ())), preferred_element_type=F32)


def mm_tn(a, b):
    return lax.dot_general(a, b, (((0,), (0,)), ((), ())), preferred_element_type=F32)


def lanes(start, size):
    return pl.ds(pl.multiple_of(start, 128), size)


def gelu_cdf(u):
    return 0.5 + 0.5 * lax.erf(u * (2.0**-0.5))


def gelu_slope(u, phi):
    return phi + u * ((2.0 * math.pi) ** -0.5) * jnp.exp(-0.5 * u * u)


def norm_stats(x):
    center = x - jnp.mean(x, axis=-1, keepdims=True)
    inverse = lax.rsqrt(jnp.mean(center * center, axis=-1, keepdims=True) + NORM_EPS)
    return center * inverse, inverse


def norm_back(up, unit, inverse, gain):
    e = up * gain
    return inverse * (
        e - jnp.mean(e, axis=-1, keepdims=True) - unit * jnp.mean(e * unit, axis=-1, keepdims=True)
    )


def attend_kernel(
    tm_ref, to_ref, wm_ref, wo_ref, vec_ref, hot_ref, msk_ref,
    qkv_ref, keep_ref, send_ref, tr_ref, ctx_ref,
):
    s = lax.axis_index("seq")
    half, width = tm_ref.shape
    own = width // 2
    mine, other = lanes(s * own, own), lanes((1 - s) * own, own)
    for j in range(3):
        w_m = wm_ref[:, lanes(j * width + s * own, own)]
        w_o = wo_ref[:, j * own : (j + 1) * own]
        for b, rows in enumerate((tm_ref, to_ref)):
            acc = mm(rows[:, mine], w_m) + mm(rows[:, other], w_o)
            if j != 1:
                acc = acc + vec_ref[6 + j // 2 : 7 + j // 2, mine]
            qkv_ref[b * half : (b + 1) * half, j * own : (j + 1) * own] = acc.astype(BF)
    hot = hot_ref[...]
    tr_ref[...] = (mm(hot[:, :half], tm_ref[...]) + mm(hot[:, half:], to_ref[...])).astype(BF)
    length = 2 * half
    valid = msk_ref[...] > 0.0
    ones = jnp.ones((length, 128), BF)
    low = lax.broadcasted_iota(jnp.int32, (1, 128), 1) < HEAD_DIM
    for pair in range(own // 128):
        at = pair * 128
        keys = qkv_ref[:, own + at : own + at + 128]
        vals = jnp.concatenate([qkv_ref[:, 2 * own + at : 2 * own + at + 128], ones], axis=1)
        for b in range(2):
            q2 = qkv_ref[b * half : (b + 1) * half, at : at + 128] * jnp.array(HEAD_DIM**-0.5, BF)
            parts = []
            for e in range(2):
                q = jnp.where(low if e == 0 else ~low, q2, jnp.zeros_like(q2))
                scores = jnp.where(valid, mm_nt(q, keys), MASKED)
                top = jnp.max(scores, axis=-1, keepdims=True)
                weights = jnp.exp(scores - top).astype(BF)
                mixed = mm(weights, vals)
                parts.append(mixed[:, :128] / mixed[:, 128:])
            ctx_ref[b * half : (b + 1) * half, at : at + 128] = jnp.where(
                low, parts[0], parts[1]
            ).astype(BF)
    rows = mm(hot, ctx_ref[...]).astype(BF)
    keep_ref[:half] = ctx_ref[:half]
    send_ref[:half] = ctx_ref[half:]
    keep_ref[half:] = rows
    send_ref[half:] = rows


def feed_kernel(
    count_ref, keep_ref, recv_ref, tm_ref, tr_ref, wout_m, wout_o, wup_m, wup_o, wdn_m, wdn_o,
    vec_ref, upb_ref, grad_ref,
    out_ref, fac_ref, dat_ref, dh1_ref, dctx_ref, sums_ref,
    ab_ref, acc_ref, slope_ref, a_ref, da_ref,
):
    s = lax.axis_index("seq")
    half, width = tm_ref.shape
    own = width // 2
    total = keep_ref.shape[0]
    ff_own = wdn_m.shape[0]
    step = ff_own // 2
    mine, other = lanes(s * own, own), lanes((1 - s) * own, own)
    out_bias, gain1, shift1 = vec_ref[0:1], vec_ref[1:2], vec_ref[2:3]
    down_bias, gain2, shift2 = vec_ref[3:4], vec_ref[4:5], vec_ref[5:6]
    attn = mm(keep_ref[...], wout_m[...]) + mm(recv_ref[...], wout_o[...]) + out_bias
    tok = jnp.concatenate([tm_ref[...], tr_ref[...]], axis=0).astype(F32)
    unit1, inv1 = norm_stats(tok + attn)
    a = unit1 * gain1 + shift1
    a_ref[...] = a
    ab_ref[...] = a.astype(BF)
    unit1_r, inv1_r = unit1[half:], inv1[half:]
    acc_ref[...] = a + down_bias
    for part, (down, base) in enumerate(((wdn_m, s * ff_own), (wdn_o, (1 - s) * ff_own))):
        for c in range(ff_own // step):
            cols = lanes(base + c * step, step)
            u = mm(ab_ref[:, mine], wup_m[:, cols]) + mm(ab_ref[:, other], wup_o[:, cols])
            u = u + upb_ref[:, cols]
            phi = gelu_cdf(u)
            g = (u * phi).astype(BF)
            k = part * ff_own + c * step
            slope_ref[:, k : k + step] = gelu_slope(u[half:], phi[half:])
            acc_ref[...] += mm(g, down[c * step : (c + 1) * step])
    unit2, inv2 = norm_stats(acc_ref[...])
    out_ref[...] = (unit2[:half] * gain2 + shift2).astype(BF)
    unit2_r, inv2_r = unit2[half:], inv2[half:]
    slots = grad_ref.shape[0]
    used = lax.broadcasted_iota(jnp.int32, (slots, 1), 0) < count_ref[0]
    dy = jnp.where(used, grad_ref[...].astype(F32), 0.0)
    sums_ref[5:6] = jnp.sum(dy * unit2_r, axis=0, keepdims=True)
    sums_ref[6:7] = jnp.sum(dy, axis=0, keepdims=True)
    dh2 = norm_back(dy, unit2_r, inv2_r, gain2)
    df = dh2.astype(BF)
    for h in range(2):
        fac_ref[0, h] = ab_ref[half:, h * own : (h + 1) * own]
        fac_ref[1, h] = df[:, h * own : (h + 1) * own]
    da_m = jnp.zeros((slots, own), F32)
    da_o = jnp.zeros((slots, own), F32)
    for part, (down, base) in enumerate(((wdn_m, s * ff_own), (wdn_o, (1 - s) * ff_own))):
        for c in range(ff_own // step):
            cols = lanes(base + c * step, step)
            k = part * ff_own + c * step
            dg = mm_nt(df, down[c * step : (c + 1) * step])
            du = (dg * slope_ref[:, k : k + step]).astype(BF)
            da_m = da_m + mm_nt(du, wup_m[:, cols])
            da_o = da_o + mm_nt(du, wup_o[:, cols])
    da_ref[:, mine] = da_m
    da_ref[:, other] = da_o
    da = dh2 + da_ref[...]
    sums_ref[3:4] = jnp.sum(da * unit1_r, axis=0, keepdims=True)
    sums_ref[4:5] = jnp.sum(da, axis=0, keepdims=True)
    dh1 = norm_back(da, unit1_r, inv1_r, gain1)
    dat = dh1.astype(BF)
    sums_ref[2:3] = jnp.sum(dat.astype(F32), axis=0, keepdims=True)
    sums_ref[0:2] = jnp.zeros((2, width), F32)
    sums_ref[7:8] = jnp.zeros((1, width), F32)
    dh1_ref[...] = dh1
    dat_ref[...] = dat
    dctx_ref[...] = mm_nt(dat, wout_m[...]).astype(BF)


def back_kernel(
    qkv_ref, hot_ref, msk_ref, dctx_ref, tm_ref, to_ref, tr_ref, keep_ref, dat_ref, wm_ref, wo_ref,
    dh1_ref, sums_ref,
    load_ref, dkeep_ref, dsend_ref, small_ref,
    dp_ref, part_ref,
):
    s = lax.axis_index("seq")
    half, width = tm_ref.shape
    own = width // 2
    length = 2 * half
    slots = dctx_ref.shape[0]
    mine, other = lanes(s * own, own), lanes((1 - s) * own, own)
    scale = HEAD_DIM**-0.5
    hot = hot_ref[...]
    valid = msk_ref[...] > 0.0
    low = lax.broadcasted_iota(jnp.int32, (1, 128), 1) < HEAD_DIM
    q_rows = (mm(hot, qkv_ref[:, :own]) * scale).astype(BF)
    dq = []
    for pair in range(own // 128):
        at = pair * 128
        keys = qkv_ref[:, own + at : own + at + 128]
        vals = qkv_ref[:, 2 * own + at : 2 * own + at + 128]
        q2, c2 = q_rows[:, at : at + 128], dctx_ref[:, at : at + 128]
        zero = jnp.zeros_like(q2)
        q4 = jnp.concatenate([jnp.where(low, q2, zero), jnp.where(low, zero, q2)], axis=0)
        c4 = jnp.concatenate([jnp.where(low, c2, zero), jnp.where(low, zero, c2)], axis=0)
        scores = jnp.where(valid, mm_nt(q4, keys), MASKED)
        probs = jnp.exp(scores - jnp.max(scores, axis=-1, keepdims=True))
        probs = probs / jnp.sum(probs, axis=-1, keepdims=True)
        dprobs = mm_nt(c4, vals)
        ds = probs * (dprobs - jnp.sum(probs * dprobs, axis=-1, keepdims=True))
        ds = ds.astype(BF)
        r = mm(ds, keys) * scale
        dq.append(jnp.where(low, r[:slots], r[slots:]).astype(BF))
        dp_ref[:, own + at : own + at + 128] = mm_tn(ds, q4).astype(BF)
        dp_ref[:, 2 * own + at : 2 * own + at + 128] = mm_tn(probs.astype(BF), c4).astype(BF)
    dq = jnp.concatenate(dq, axis=1)
    dp_ref[:, :own] = mm_tn(hot, dq).astype(BF)
    for side, cols in enumerate((other, mine)):
        base = side * 3 * own
        load_ref[base : base + own] = mm_tn(tr_ref[:, cols], dq).astype(BF)
        for j in (1, 2):
            g = mm_tn(tm_ref[:, cols], dp_ref[:half, j * own : (j + 1) * own])
            g = g + mm_tn(to_ref[:, cols], dp_ref[half:, j * own : (j + 1) * own])
            load_ref[base + j * own : base + (j + 1) * own] = g.astype(BF)
    for h in range(2):
        g = mm_tn(keep_ref[half:], dat_ref[:, h * own : (h + 1) * own])
        load_ref[(6 + h) * own : (7 + h) * own] = g.astype(BF)
    if load_ref.shape[0] > 8 * own:
        load_ref[8 * own :] = jnp.zeros((load_ref.shape[0] - 8 * own, own), BF)
    p_m = jnp.zeros((length, own), F32)
    p_o = jnp.zeros((length, own), F32)
    for j in range(3):
        d = dp_ref[:, j * own : (j + 1) * own]
        p_m = p_m + mm_nt(d, wm_ref[:, lanes(j * width + s * own, own)])
        p_o = p_o + mm_nt(d, wo_ref[:, j * own : (j + 1) * own])
    part_ref[:, mine] = p_m
    part_ref[:, other] = p_o
    dh1 = dh1_ref[...]
    high = dh1.astype(BF)
    rest = (dh1 - high.astype(F32)).astype(BF)
    near = hot[:, :half]
    dkeep_ref[...] = part_ref[:half] + mm_tn(near, high) + mm_tn(near, rest)
    dsend_ref[...] = part_ref[half:].astype(BF)
    small_ref[...] = sums_ref[:, mine]
    small_ref[0:1] = jnp.sum(dq.astype(F32), axis=0, keepdims=True)
    small_ref[1:2] = jnp.sum(dp_ref[:, 2 * own :].astype(F32), axis=0, keepdims=True)


class Plan:
    def __init__(self, mesh, rows):
        axis = mesh.axis_names.index("batch")
        line = np.moveaxis(mesh.devices, axis, 0)
        line = line.reshape(line.shape[0], -1)[:, 0]
        n = len(line)
        self.n = n
        dims = []
        try:
            coords = [tuple(d.coords) for d in line]
            for d in range(3):
                size = len({c[d] for c in coords})
                if size > 1:
                    first = coords[0]
                    stride = next(
                        i
                        for i, c in enumerate(coords)
                        if c[d] != first[d] and all(c[e] == first[e] for e in range(3) if e != d)
                    )
                    dims.append((size, stride))
            good = all(
                c[d] >= 0 for c in coords for d in range(3)
            ) and math.prod(size for size, _ in dims) == n
            if not good:
                dims = []
        except (AttributeError, StopIteration):
            dims = []
        if not dims:
            rest, stride = n, 1
            while rest > 1:
                dims.append((2 if rest % 2 == 0 else rest, stride))
                stride *= dims[-1][0]
                rest //= dims[-1][0]
        dims.sort()
        self.orders = [dims]
        if len(dims) > 1:
            self.orders.append([dims[1], dims[0]] + dims[2:])
        self.peers = [(size, stride, o) for size, stride in dims for o in range(1, size)]
        unit = 16 * n
        streams = max(2, min(4, rows // unit))
        streams += streams % 2
        self.piece = -(-rows // (streams * unit)) * 16
        self.streams = streams
        self.rows = streams * n * self.piece
        self.copies = sum(size - 1 for size, _ in dims)


def coordinate(me, size, stride):
    return lax.rem(lax.div(me, stride), size)


def peer_of(me, size, stride, offset):
    here = coordinate(me, size, stride)
    there = lax.rem(here + offset, size)
    return me + (there - here) * stride, there


def reduce_kernel(
    plan, load_ref, fac_ref, small_ref,
    res_ref, got_ref, gath_ref, total_ref,
    buf_ref, in_ref, sm_ref,
    rs_send, rs_recv, ag_send, ag_recv, fa_send, fa_recv, fw_send, fw_recv, ow_send, ow_recv, sm_send, sm_recv, x_send, x_recv,
):
    me = lax.axis_index("batch")
    s = lax.axis_index("seq")
    n, piece = plan.n, plan.piece

    barrier = pltpu.get_barrier_semaphore()
    for size, stride, o in plan.peers:
        to, _ = peer_of(me, size, stride, o)
        pl.semaphore_signal(barrier, inc=1, device_id={"batch": to}, device_id_type=MESH)
    pl.semaphore_signal(barrier, inc=1, device_id={"seq": 1 - s}, device_id_type=MESH)
    pl.semaphore_wait(barrier, len(plan.peers) + 1)

    def copy(src, dst, send, recv, where):
        return pltpu.make_async_remote_copy(
            src_ref=src, dst_ref=dst, send_sem=send, recv_sem=recv, device_id=where,
            device_id_type=MESH,
        )

    def place(order):
        spots, base, span = [], jnp.int32(0), n
        for size, stride in order:
            span //= size
            spots.append((base, span))
            base = base + coordinate(me, size, stride) * span
        return spots, base

    places = [place(order) for order in plan.orders]
    pending = []

    def window(h, done, moved=None, there=None):
        spots = []
        for dim in plan.orders[0]:
            if dim == moved:
                spots.append(pl.ds(there, 1))
            elif dim in done:
                spots.append(pl.ds(0, dim[0]))
            else:
                spots.append(pl.ds(coordinate(me, *dim), 1))
        return gath_ref.at[(s, h, *spots)]

    unit = (1,) * len(plan.orders[0])
    for h in range(2):
        here = tuple(pl.ds(coordinate(me, *dim), 1) for dim in plan.orders[0])
        gath_ref[(pl.ds(s, 1), pl.ds(h, 1), *here)] = fac_ref[pl.ds(s, 1), h].reshape(
            (1, 1) + unit + fac_ref.shape[2:]
        )

    def gather_stage(level):
        started = []
        for h in range(2):
            order = plan.orders[h % len(places)]
            dim, done = order[level], order[level + 1 :]
            size, stride = dim
            here = coordinate(me, size, stride)
            for o in range(1, size):
                to, _ = peer_of(me, size, stride, o)
                sem = (h, level, o - 1)
                block = window(h, done)
                c = copy(block, block, fa_send.at[sem], fa_recv.at[sem], {"batch": to})
                c.start()
                back = lax.rem(here + size - o, size)
                started.append((c, h, level, o, window(h, done, dim, back)))
        return started

    def gather_finish(started):
        for c, h, level, o, theirs in started:
            c.wait_recv()
            sem = (h, level, o - 1)
            f = copy(
                theirs, theirs, fw_send.at[sem], fw_recv.at[sem], {"seq": 1 - s}
            )
            f.start()
            pending.append(c.wait_send)
            pending.append(f.wait)

    def reduce_start(stream, level):
        w = stream % len(places)
        order = plan.orders[w]
        base, span = places[w][0][level]
        size, stride = order[level]
        off = stream * n * piece
        ops = []
        count = sum(z - 1 for z, _ in order[:level])
        for o in range(1, size):
            to, there = peer_of(me, size, stride, o)
            src = load_ref if level == 0 else buf_ref
            at = pl.ds(pl.multiple_of(off + (base + there * span) * piece, 16), span * piece)
            slot = pl.ds(in_base(stream, level) + (o - 1) * span * piece, span * piece)
            sem = (stream, count + o - 1)
            c = copy(src.at[at], in_ref.at[slot], rs_send.at[sem], rs_recv.at[sem], {"batch": to})
            c.start()
            ops.append(c)
        return ops

    def in_base(stream, level):
        order = plan.orders[stream % len(places)]
        rows, span = 0, n
        for size, _ in order[:level]:
            span //= size
            rows += (size - 1) * span
        return (stream * n + rows) * piece

    def reduce_finish(stream, level, ops):
        w = stream % len(places)
        order = plan.orders[w]
        base, span = places[w][0][level]
        size, stride = order[level]
        off = stream * n * piece
        for c in ops:
            c.wait()
        here = coordinate(me, size, stride)
        at = pl.ds(pl.multiple_of(off + (base + here * span) * piece, 16), span * piece)
        src = load_ref if level == 0 else buf_ref
        acc = src[at].astype(F32)
        for o in range(1, size):
            slot = pl.ds(in_base(stream, level) + (o - 1) * span * piece, span * piece)
            acc = acc + in_ref[slot].astype(F32)
        dst = res_ref if level == len(order) - 1 else buf_ref
        dst[at] = acc.astype(BF)

    def spread_start(stream, level):
        w = stream % len(places)
        order = plan.orders[w]
        base, span = places[w][0][level]
        size, stride = order[level]
        off = stream * n * piece
        here = coordinate(me, size, stride)
        at = pl.ds(pl.multiple_of(off + (base + here * span) * piece, 16), span * piece)
        count = sum(z - 1 for z, _ in order[:level])
        ops = []
        for o in range(1, size):
            to, _ = peer_of(me, size, stride, o)
            sem = (stream, count + o - 1)
            c = copy(res_ref.at[at], res_ref.at[at], ag_send.at[sem], ag_recv.at[sem], {"batch": to})
            c.start()
            ops.append(c)
        return ops

    def small_start(level, value):
        size, stride = plan.orders[0][level]
        here = coordinate(me, size, stride)
        first = sum(z for z, _ in plan.orders[0][:level])
        sm_ref[pl.ds(first + here, 1)] = value[None]
        ops = []
        for o in range(1, size):
            to, _ = peer_of(me, size, stride, o)
            sem = first + o
            slot = pl.ds(first + here, 1)
            c = copy(sm_ref.at[slot], sm_ref.at[slot], sm_send.at[sem], sm_recv.at[sem], {"batch": to})
            c.start()
            ops.append(c)
        return ops

    def small_finish(level, ops):
        for c in ops:
            c.wait()
        size, _ = plan.orders[0][level]
        first = sum(z for z, _ in plan.orders[0][:level])
        acc = sm_ref[first]
        for o in range(1, size):
            acc = acc + sm_ref[first + o]
        return acc

    levels = len(plan.orders[0])
    last = levels - 1
    running = {t: reduce_start(t, 0) for t in range(plan.streams)}
    gathers = gather_stage(last)
    for h in range(2):
        own_copy = copy(
            window(h, ()), window(h, ()), ow_send.at[h], ow_recv.at[h], {"seq": 1 - s}
        )
        own_copy.start()
        pending.append(own_copy.wait)
    small = small_ref[...]
    for level in range(levels):
        small_ops = small_start(level, small)
        gather_finish(gathers)
        gathers = gather_stage(last - 1 - level) if level < last else []
        for t in range(plan.streams):
            reduce_finish(t, level, running[t])
            running[t] = reduce_start(t, level + 1) if level < last else spread_start(t, last)
        small = small_finish(level, small_ops)
    total_ref[...] = small
    cross = got_ref.shape[0]
    span = n * piece
    for level in range(last, -1, -1):
        for t in range(plan.streams):
            for c in running[t]:
                c.wait()
            if level > 0:
                running[t] = spread_start(t, level - 1)
            elif t * span < cross:
                rows = pl.ds(t * span, min(span, cross - t * span))
                x = copy(res_ref.at[rows], got_ref.at[rows], x_send.at[t], x_recv.at[t], {"seq": 1 - s})
                x.start()
                pending.append(x.wait)
    for wait in pending:
        wait()


def ffn_kernel(
    gath_ref, wup_m, wup_o, wdn_m, upb_ref,
    gdn_ref, gup_ref, gsend_ref, bias_ref, dbias_ref,
    far_ref,
):
    s = lax.axis_index("seq")
    step, steps = pl.program_id(0), pl.num_programs(0)
    own = gath_ref.shape[3]
    ff_own = wdn_m.shape[0]
    size = 512 if ff_own % 512 == 0 else ff_own
    sides = pl.ds(s, 1), pl.ds(1 - s, 1)

    @pl.when(step == 0)
    def _():
        for ref in (gdn_ref, gup_ref, far_ref, bias_ref, dbias_ref):
            ref[...] = jnp.zeros_like(ref)

    for h in range(2):
        dbias_ref[h : h + 1] += jnp.sum(gath_ref[1, h].astype(F32), axis=0, keepdims=True)
    for c in range(ff_own // size):
        cols = lanes(s * ff_own + c * size, size)
        at = slice(c * size, (c + 1) * size)
        u = mm(gath_ref[0, sides[0]][0], wup_m[:, cols])
        u = u + mm(gath_ref[0, sides[1]][0], wup_o[:, cols]) + upb_ref[:, cols]
        phi = gelu_cdf(u)
        g = (u * phi).astype(BF)
        dg = mm_nt(gath_ref[1, 0], wdn_m[at, :own]) + mm_nt(gath_ref[1, 1], wdn_m[at, own:])
        du = (dg * gelu_slope(u, phi)).astype(BF)
        bias_ref[:, at] += jnp.sum(du.astype(F32), axis=0, keepdims=True)
        for h in range(2):
            gdn_ref[at, h * own : (h + 1) * own] += mm_tn(g, gath_ref[1, h])
        gup_ref[:, at] += mm_tn(gath_ref[0, sides[0]][0], du)
        far_ref[:, at] += mm_tn(gath_ref[0, sides[1]][0], du)

    @pl.when(step == steps - 1)
    def _():
        gsend_ref[...] = far_ref[...].astype(BF)


def final_kernel(res_ref, got_ref, gup_ref, grecv_ref, gqkv_out, gout_out, gup_out):
    s = lax.axis_index("seq")
    own = gout_out.shape[0]
    width, ff_own = 2 * own, gup_ref.shape[1]
    for j in range(3):
        gqkv_out[:, lanes(j * width + s * own, own)] = res_ref[(3 + j) * own : (4 + j) * own].astype(F32)
        gqkv_out[:, lanes(j * width + (1 - s) * own, own)] = got_ref[j * own : (j + 1) * own].astype(F32)
    for h in range(2):
        gout_out[:, h * own : (h + 1) * own] = res_ref[(6 + h) * own : (7 + h) * own].astype(F32)
    gup_out[:, lanes(s * ff_own, ff_own)] = gup_ref[...]
    gup_out[:, lanes((1 - s) * ff_own, ff_own)] = grecv_ref[...].astype(F32)


def shape(dims, kind=BF):
    return jax.ShapeDtypeStruct(dims, kind)


def local_call(kernel, outs, scratch=(), scalars=0, args=0):
    extra = {}
    if scalars:
        extra["in_specs"] = [pl.BlockSpec(memory_space=pltpu.SMEM)] * scalars + [
            pl.BlockSpec(memory_space=pltpu.VMEM)
        ] * (args - scalars)
    return pl.pallas_call(
        kernel,
        out_shape=outs,
        scratch_shapes=scratch,
        compiler_params=pltpu.CompilerParams(vmem_limit_bytes=VMEM_LIMIT),
        **extra,
    )


def body(
    mesh, tokens, w_qkv, q_bias, v_bias, w_out, out_bias, attn_gain, attn_shift, w_up, up_bias,
    w_down, down_bias, ffn_gain, ffn_shift, seq_len, grad_pos, grad_count, out_grad,
):
    half, width = tokens.shape[1:]
    own, ff_own = w_qkv.shape[0], w_down.shape[0]
    length, slots, ff = 2 * half, grad_pos.shape[1], 2 * ff_own
    plan = Plan(mesh, 8 * own)
    n = plan.n
    s = lax.axis_index("seq")
    swap = lambda x: lax.ppermute(x, "seq", [(0, 1), (1, 0)])
    tm = tokens[0]
    cols = jnp.concatenate(
        [lax.dynamic_slice_in_dim(w_qkv, j * width + (1 - s) * own, own, 1) for j in range(3)], axis=1
    )
    to, wqkv_o = swap(tm), swap(cols)
    wout_o, wup_o, wdn_o = swap(w_out), swap(w_up), swap(w_down)
    vec = jnp.stack(
        [out_bias, attn_gain, attn_shift, down_bias, ffn_gain, ffn_shift, q_bias, v_bias]
    )
    upb = up_bias.reshape(1, ff)
    row = jnp.arange(length, dtype=jnp.int32)
    pos = jnp.where(row < half, row + s * half, row - half + (1 - s) * half)
    live = jnp.arange(slots)[:, None] < grad_count[0]
    hot = ((grad_pos[0][:, None] == pos[None, :]) & live).astype(BF)
    msk = (pos < seq_len[0]).astype(F32)[None]

    qkv, keep, send, tr = local_call(
        attend_kernel,
        [shape((length, 3 * own)), shape((half + slots, own)), shape((half + slots, own)),
         shape((slots, width))],
        [pltpu.VMEM((length, own), BF)],
    )(tm, to, w_qkv, wqkv_o, vec, hot, msk)
    recv = swap(send)
    out, fac, dat, dh1, dctx, sums = local_call(
        feed_kernel,
        [shape((half, width)), shape((2, 2, slots, own)), shape((slots, width)),
         shape((slots, width), F32), shape((slots, own)), shape((8, width), F32)],
        [pltpu.VMEM((half + slots, width), BF), pltpu.VMEM((half + slots, width), F32),
         pltpu.VMEM((slots, ff), F32), pltpu.VMEM((half + slots, width), F32),
         pltpu.VMEM((slots, width), F32)],
        scalars=1, args=14,
    )(grad_count, keep, recv, tm, tr, w_out, wout_o, w_up, wup_o, w_down, wdn_o, vec, upb, out_grad[0])
    load, dkeep, dsend, small = local_call(
        back_kernel,
        [shape((plan.rows, own)), shape((half, width), F32), shape((half, width)),
         shape((8, own), F32)],
        [pltpu.VMEM((length, 3 * own), BF), pltpu.VMEM((length, width), F32)],
    )(qkv, hot, msk, dctx, tm, to, tr, keep, dat, w_qkv, wqkv_o, dh1, sums)
    drecv = swap(dsend)
    grad_tok = (dkeep + drecv.astype(F32)).astype(BF)[None]

    dma = pltpu.SemaphoreType.DMA
    depth, widest = len(plan.orders[0]), max(size for size, _ in plan.orders[0]) - 1
    slots_small = sum(size for size, _ in plan.orders[0])
    cross = 3 * own
    res, got, gath, total = pl.pallas_call(
        functools.partial(reduce_kernel, plan),
        out_shape=[shape((plan.rows, own)), shape((cross, own)), shape((2, 2, *(size for size, _ in plan.orders[0]), slots, own)),
                   shape((8, own), F32)],
        scratch_shapes=[
            pltpu.VMEM((plan.rows, own), BF), pltpu.VMEM((plan.rows, own), BF),
            pltpu.VMEM((slots_small, 8, own), F32),
            dma((plan.streams, plan.copies)), dma((plan.streams, plan.copies)),
            dma((plan.streams, plan.copies)), dma((plan.streams, plan.copies)),
            dma((2, depth, widest)), dma((2, depth, widest)),
            dma((2, depth, widest)), dma((2, depth, widest)),
            dma((2,)), dma((2,)),
            dma((slots_small,)), dma((slots_small,)),
            dma((plan.streams,)), dma((plan.streams,)),
        ],
        compiler_params=pltpu.CompilerParams(
            collective_id=0, has_side_effects=True, vmem_limit_bytes=VMEM_LIMIT
        ),
    )(load, fac, small)

    rows = n * slots
    tile = rows if rows <= 1280 else 1280 if rows % 1280 == 0 else slots
    fixed = lambda *dims: pl.BlockSpec(dims, lambda i: (0,) * len(dims), pipeline_mode=pl.Buffered(1))
    gdn, gup, gsend, ubias, dbias = pl.pallas_call(
        ffn_kernel,
        grid=(rows // tile,),
        in_specs=[pl.BlockSpec((2, 2, tile, own), lambda i: (0, 0, i, 0)), fixed(own, ff),
                  fixed(own, ff), fixed(ff_own, width), fixed(1, ff)],
        out_specs=[fixed(ff_own, width), fixed(own, ff_own), fixed(own, ff_own), fixed(1, ff_own),
                   fixed(2, own)],
        out_shape=[shape((ff_own, width), F32), shape((own, ff_own), F32), shape((own, ff_own)),
                   shape((1, ff_own), F32), shape((2, own), F32)],
        scratch_shapes=[pltpu.VMEM((own, ff_own), F32)],
        compiler_params=pltpu.CompilerParams(vmem_limit_bytes=VMEM_LIMIT),
    )(gath.reshape(2, 2, rows, own), w_up, wup_o, w_down, upb)
    grecv = swap(gsend)
    gqkv, gout, gup = local_call(
        final_kernel,
        [shape((own, 3 * width), F32), shape((own, width), F32), shape((own, ff), F32)],
    )(res, got, gup, grecv)
    return (
        out[None], grad_tok, gqkv, total[0], total[1], gout, total[2], total[3], total[4], gup,
        ubias[0], gdn, lax.dynamic_index_in_dim(dbias, s, 0, keepdims=False), total[5], total[6],
    )


def solution(mesh):
    specs = dict(
        in_specs=(
            P("batch", "seq", None), P("seq", None), P(), P(), P("seq", None), P(), P(), P(),
            P("seq", None), P(), P("seq", None), P(), P(), P(), P("batch"), P("batch", None),
            P("batch"), P("batch", None, None),
        ),
        out_specs=(
            P("batch", "seq", None), P("batch", "seq", None), P("seq", None), P("seq"), P("seq"),
            P("seq", None), P("seq"), P("seq"), P("seq"), P("seq", None), P("seq"),
            P("seq", None), P("seq"), P("seq"), P("seq"),
        ),
    )
    return jax.shard_map(functools.partial(body, mesh), mesh=mesh, check_vma=False, **specs)
```

time: 821 us -> 160 us (0.19); the launches traced: 812 us -> 159 us
  blocking collectives: 630 us -> 0 us
  Pallas kernels: 0 us -> 141 us
  matrix products: 60.9 us -> 0 us
  waiting for transfers between devices: 36.9 us -> 5.54 us
  local copies, waits for them, and re-layouts: 35 us -> 4.73 us
  other arithmetic: 21.1 us -> 3.53 us
  between operations: 17.7 us -> 2.22 us
    psum x1 -> x0, blocking collectives: 608 us -> none  [body(): lax.psum((total_w_qkv, total_q_bias, total_v_bias, total_w_out, total_out...]
    pallas_call x0 -> x6, Pallas kernels: none -> 141 us  [the longest x1 78.6 us: body(): pl.pallas_call(functools.partial(reduce_kernel, plan), out_shape=[shape((...]
    dot_general x19 -> x0, matrix products: 60.9 us -> none  [the longest x1 11.3 us: body(): jnp.dot(normed_low, full_up, preferred_element_type=jnp.float32) + up_bias]
    reduce_scatter x3 -> x0, waiting for transfers between devices: 19.8 us -> none  [the longest x1 16.7 us: body(): lax.psum_scatter(grad_w_down.astype(jnp.bfloat16), 'seq', scatter_dimensi...]
    unnamed x91 -> x28, local copies, waits for them, and re-layouts: 21.2 us -> 1.48 us
    all_to_all x4 -> x0, blocking collectives: 18.3 us -> none  [the longest x1 5 us: body(): lax.all_to_all(packed.reshape(seq_local, half_len, 3, model_width), 'seq'...]
    all_gather x4 -> x0, waiting for transfers between devices: 14.5 us -> none  [the longest x1 13.2 us: body(): lax.all_gather(w_qkv, 'seq', axis=0, tiled=True)]
    unnamed x1 -> x0, starting transfers between devices: 10 us -> none
  transfers between devices with their start and end apart: 8 -> 8, of which waited for: 4 -> 3; matrix products, arithmetic and copies ran while one was open for 10% -> 4% of each run, Pallas kernels for 0% -> 4%
where the time goes in v1:
time: 160 us; the launch traced here: 159 us
  Pallas kernels  141 us (88%)
  waiting for transfers between devices  5.54 us (3%)
  local copies, waits for them, and re-layouts  4.73 us (3%)
  other arithmetic  3.53 us (2%)
  starting transfers between devices  2.53 us (2%)
  between operations  2.22 us (1%)
    pallas_call x1, Pallas kernels, body(): pl.pallas_call(functools.partial(reduce_kernel, plan), out_shape=[shape((...  78.6 us
    pallas_call x1, Pallas kernels, body(): pl.pallas_call(ffn_kernel, grid=(rows // tile,), in_specs=[pl.BlockSpec((...  24.8 us
    pallas_call x1, Pallas kernels, body(): local_call(feed_kernel, [shape((half, width)), shape((2, 2, slots, own)),...  14.2 us
    pallas_call x1, Pallas kernels, body(): local_call(back_kernel, [shape((plan.rows, own)), shape((half, width), F3...  9.04 us
    pallas_call x1, Pallas kernels, body(): local_call(final_kernel, [shape((own, 3 * width), F32), shape((own, width...  7.28 us
    pallas_call x1, Pallas kernels, body(): local_call(attend_kernel, [shape((length, 3 * own)), shape((half + slots,...  6.82 us
    ppermute x8, waiting for transfers between devices, body(): swap = lambda x: lax.ppermute(x, 'seq', [(0, 1), (1, 0)])  5.54 us
  transfers between devices with their start and end apart: 8, of which 3 were waited for; matrix products, arithmetic and copies ran while one was open for 4% of the time, Pallas kernels for 4%

profile of v1, /device:TPU:0, one launch (start us, length us, event | category | flops | bytes accessed | tf_op | source)
XLA Modules:
  0.0 159.3 jit_solution(8206370910429507071)
XLA Ops:
  0.6 0.0 copy-start
  0.7 0.0 copy-start.5
  0.7 0.0 copy-start.6
  0.7 0.0 copy-start.7
  0.7 0.0 copy-start.8
  0.7 0.0 copy-start.9
  0.7 0.0 copy-start.10
  0.7 0.0 copy-start.11
  0.7 0.0 copy-start.12
  0.7 0.0 copy-start.13
  0.8 0.6 collective-permute-start.4
  1.3 0.1 collective-permute-start.5
  1.4 1.2 constant_dynamic-slice_fusion.2
  2.6 0.1 pad_maximum_fusion
  2.7 0.5 collective-permute-start.1
  3.2 0.0 copy-done
  3.2 0.1 collective-permute-start
  3.3 0.4 collective-permute-start.3
  4.4 0.6 compare_convert_fusion.msk_ref
  5.6 0.0 copy-done.5
  5.7 0.0 copy-done.6
  5.7 0.0 copy-done.7
  5.7 0.0 copy-done.8
  5.7 0.0 copy-done.9
  5.7 0.0 copy-done.10
  5.8 0.0 copy-done.11
  5.8 0.0 copy-done.12
  5.8 0.7 stack.35.vec_ref
  6.5 0.0 copy-done.13
  6.5 0.7 and_convert_fusion.hot_ref
  7.2 3.7 %collective-permute-done.to_ref = bf16[256,768]{1,0:T(8,128)(2,1)S(1)} collective-permute-done((bf16[256,768]{1,0:T(8,128)(2,1)S(1)}, bf16[256,768]{1,0:T(8,128)(2,1)S(1)}, u32[]{:S(2)}, u32[]{:S(2)}) %collective-permute-start) | collective-permute-done | bytes 393248 | tf_op jit(solution)/shard_map/ppermute | solution.py:587
  10.9 0.0 copy-start.1
  10.9 0.0 collective-permute-done.1.wo_ref
  10.9 0.7 copy-done.1
  11.6 6.8 %shard_map.289 = (bf16[512,1152]{1,0:T(8,128)(2,1)}, bf16[336,384]{1,0:T(8,128)(2,1)}, bf16[336,384]{1,0:T(8,128)(2,1)}, bf16[80,768]{1,0:T(8,128)(2,1)}) custom-call(bf16[256,768]{1,0:T(8,128)(2,1)} %bitcast.13, bf16[256,768]{1,0:T(8,128)(2,1)} %copy-done.1, bf16[384,2304]{1,0:T(8,128)(2,1)} %wm_ref.3, bf16[384,1152]{1,0:T(8,128)(2,1)} %collective-permute-done.1.wo_ref, ...), custom_call_target="tpu_custom_call" | custom-call | tf_op jit(solution)/shard_map/pallas_call | solution.py:604
  18.4 0.4 collective-permute-start.2
  18.8 0.0 collective-permute-done.3.wout_o
  18.8 1.4 collective-permute-done.2.recv_ref
  20.2 0.0 copy-start.3
  20.2 0.0 collective-permute-done.4.wup_o
  20.2 0.0 collective-permute-done.5.wdn_o
  20.2 0.7 copy-done.3
  20.9 14.2 %shard_map.290 = (bf16[256,768]{1,0:T(8,128)(2,1)}, bf16[2,2,80,384]{3,2,1,0:T(8,128)(2,1)}, bf16[80,768]{1,0:T(8,128)(2,1)}, f32[80,768]{1,0:T(8,128)}, bf16[80,384]{1,0:T(8,128)(2,1)}, /*index=5*/f32[8,768]{1,0:T(8,128)}) custom-call(s32[1]{0:T(128)} %copy.34.count_ref, bf16[336,384]{1,0:T(8,128)(2,1)} %get-tuple-element.41.keep_ref, ...), custom_call_target="tpu_custom_call" | custom-call | tf_op jit(solution)/shard_map/pallas_call | solution.py:611
  35.1 9.0 %shard_map.291 = (bf16[3072,384]{1,0:T(8,128)(2,1)}, f32[256,768]{1,0:T(8,128)}, bf16[256,768]{1,0:T(8,128)(2,1)}, f32[8,384]{1,0:T(8,128)}) custom-call(bf16[512,1152]{1,0:T(8,128)(2,1)} %get-tuple-element.45.qkv_ref, bf16[80,512]{1,0:T(8,128)(2,1)} %and_convert_fusion.hot_ref, f32[1,512]{1,0:T(1,128)} %compare_convert_fusion.msk_ref, ...), custom_call_target="tpu_custom_call" | custom-call | tf_op jit(solution)/shard_map/pallas_call | solution.py:620
  44.2 78.6 %shard_map.292 = (bf16[3072,384]{1,0:T(8,128)(2,1)}, bf16[1152,384]{1,0:T(8,128)(2,1)}, bf16[2,2,2,2,4,80,384]{6,5,4,3,2,1,0:T(8,128)(2,1)}, f32[8,384]{1,0:T(8,128)}) custom-call(bf16[3072,384]{1,0:T(8,128)(2,1)} %get-tuple-element.52.load_ref, bf16[2,2,80,384]{3,2,1,0:T(8,128)(2,1)} %get-tuple-element.53.fac_ref, f32[8,384]{1,0:T(8,128)} %get-tuple-element.54.small_ref), custom_call_target="tpu_custom_call" | custom-call | tf_op jit(solution)/shard_map/pallas_call | solution.py:633
  122.8 0.0 copy-start.4
  122.8 0.0 copy-start.2
  122.8 24.8 %shard_map.293 = (f32[1536,768]{1,0:T(8,128)}, f32[384,1536]{1,0:T(8,128)}, bf16[384,1536]{1,0:T(8,128)(2,1)}, f32[1,1536]{1,0:T(1,128)}, f32[2,384]{1,0:T(2,128)}) custom-call(bf16[2,2,1280,384]{3,2,1,0:T(8,128)(2,1)} %bitcast.12, bf16[384,3072]{1,0:T(8,128)(2,1)} %wup_m.3, bf16[384,3072]{1,0:T(8,128)(2,1)} %collective-permute-done.4.wup_o, ...), custom_call_target="tpu_custom_call" | custom-call | tf_op jit(solution)/shard_map/pallas_call | solution.py:656
  147.6 0.0 collective-permute-start.7
  147.6 0.5 collective-permute-start.6
  148.1 1.3 reduce.5
  149.4 0.0 copy-done.4
  149.4 1.3 slice_reduce_fusion
  150.7 0.5 collective-permute-done.6
  151.2 0.0 copy-done.2
  151.2 0.8 fusion
  152.0 0.0 collective-permute-done.7.grecv_ref
  152.0 7.3 %shard_map.294 = (f32[384,2304]{1,0:T(8,128)}, f32[384,768]{1,0:T(8,128)}, f32[384,3072]{1,0:T(8,128)}) custom-call(bf16[3072,384]{1,0:T(8,128)(2,1)} %get-tuple-element.55.res_ref, bf16[1152,384]{1,0:T(8,128)(2,1)} %get-tuple-element.56.got_ref, f32[384,1536]{1,0:T(8,128)} %get-tuple-element.58.gup_ref, bf16[384,1536]{1,0:T(8,128)(2,1)} %collective-permute-done.7.grecv_ref), custom_call_target="tpu_custom_call" | custom-call | tf_op jit(solution)/shard_map/pallas_call | solution.py:669
  (10 shorter events, 0.0 us)
Async XLA Ops:
  0.6 2.6 %copy-start = (bf16[1,256,768]{2,1,0:T(8,128)(2,1)S(1)}, bf16[1,256,768]{2,1,0:T(8,128)(2,1)}, u32[]{:S(2)}) copy-start(bf16[1,256,768]{2,1,0:T(8,128)(2,1)} %param.18) | copy-start | bytes 1179652
  0.7 5.0 %copy-start.5 = (f32[768]{0:T(1024)S(1)}, f32[768]{0:T(1024)}, u32[]{:S(2)}) copy-start(f32[768]{0:T(1024)} %param.23) | copy-start | bytes 9220
  0.7 5.0 %copy-start.6 = (f32[768]{0:T(1024)S(1)}, f32[768]{0:T(1024)}, u32[]{:S(2)}) copy-start(f32[768]{0:T(1024)} %param.24) | copy-start | bytes 9220
  0.7 5.0 %copy-start.7 = (f32[768]{0:T(1024)S(1)}, f32[768]{0:T(1024)}, u32[]{:S(2)}) copy-start(f32[768]{0:T(1024)} %param.25) | copy-start | bytes 9220
  0.7 5.0 %copy-start.8 = (f32[768]{0:T(1024)S(1)}, f32[768]{0:T(1024)}, u32[]{:S(2)}) copy-start(f32[768]{0:T(1024)} %param.29) | copy-start | bytes 9220
  0.7 5.0 %copy-start.9 = (f32[768]{0:T(1024)S(1)}, f32[768]{0:T(1024)}, u32[]{:S(2)}) copy-start(f32[768]{0:T(1024)} %param.30) | copy-start | bytes 9220
  0.7 5.0 %copy-start.10 = (f32[768]{0:T(1024)S(1)}, f32[768]{0:T(1024)}, u32[]{:S(2)}) copy-start(f32[768]{0:T(1024)} %param.31) | copy-start | bytes 9220
  0.7 5.0 %copy-start.11 = (f32[768]{0:T(1024)S(1)}, f32[768]{0:T(1024)}, u32[]{:S(2)}) copy-start(f32[768]{0:T(1024)} %param.20) | copy-start | bytes 9220
  0.7 5.1 %copy-start.12 = (f32[768]{0:T(1024)S(1)}, f32[768]{0:T(1024)}, u32[]{:S(2)}) copy-start(f32[768]{0:T(1024)} %param.21) | copy-start | bytes 9220
  0.7 5.7 %copy-start.13 = (s32[1,80]{1,0:T(1,128)S(1)}, s32[1,80]{1,0:T(1,128)}, u32[]{:S(2)}) copy-start(s32[1,80]{1,0:T(1,128)} %param.33) | copy-start | bytes 964
  0.8 19.4 %collective-permute-start.4 = (bf16[384,3072]{1,0:T(8,128)(2,1)}, bf16[384,3072]{1,0:T(8,128)(2,1)}, u32[]{:S(2)}, u32[]{:S(2)}) collective-permute-start(bf16[384,3072]{1,0:T(8,128)(2,1)} %wup_m.3), channel_id=1, source_target_pairs={{0,16},{16,0},{1,17},{17,1},{2,18},{18,2},{3,19},{19,3},{4,20},{20... | collective-permute-start | bytes 7077896 | tf_op jit(solution)/shard_map/ppermute | solution.py:587
  1.3 18.9 %collective-permute-start.5 = (bf16[1536,768]{1,0:T(8,128)(2,1)}, bf16[1536,768]{1,0:T(8,128)(2,1)}, u32[]{:S(2)}, u32[]{:S(2)}) collective-permute-start(bf16[1536,768]{1,0:T(8,128)(2,1)} %wdn_m.3), channel_id=1, source_target_pairs={{0,16},{16,0},{1,17},{17,1},{2,18},{18,2},{3,19},{19,3},{4,20},{20... | collective-permute-start | bytes 7077896 | tf_op jit(solution)/shard_map/ppermute | solution.py:587
  2.7 8.2 %collective-permute-start.1 = (bf16[384,1152]{1,0:T(8,128)(2,1)S(1)}, bf16[384,1152]{1,0:T(8,128)(2,1)}, u32[]{:S(2)}, u32[]{:S(2)}) collective-permute-start(bf16[384,1152]{1,0:T(8,128)(2,1)S(1)} %pad_maximum_fusion), channel_id=1, source_target_pairs={{0,16},{16,0},{1,17},{17,1},{2,18},{18,2},{3,19},{19,3},{4,20},{20... | collective-permute-start | bytes 2654216 | tf_op jit(solution)/shard_map/ppermute | solution.py:587
  3.2 7.7 %collective-permute-start = (bf16[256,768]{1,0:T(8,128)(2,1)S(1)}, bf16[256,768]{1,0:T(8,128)(2,1)S(1)}, u32[]{:S(2)}, u32[]{:S(2)}) collective-permute-start(bf16[256,768]{1,0:T(8,128)(2,1)S(1)} %bitcast.16), channel_id=1, source_target_pairs={{0,16},{16,0},{1,17},{17,1},{2,18},{18,2},{3,19},{19,3},{4,20},{20... | collective-permute-start | bytes 1179656 | tf_op jit(solution)/shard_map/ppermute | solution.py:587
  3.3 15.5 %collective-permute-start.3 = (bf16[384,768]{1,0:T(8,128)(2,1)}, bf16[384,768]{1,0:T(8,128)(2,1)}, u32[]{:S(2)}, u32[]{:S(2)}) collective-permute-start(bf16[384,768]{1,0:T(8,128)(2,1)} %wout_m.1), channel_id=1, source_target_pairs={{0,16},{16,0},{1,17},{17,1},{2,18},{18,2},{3,19},{19,3},{4,20},{20... | collective-permute-start | bytes 1769480 | tf_op jit(solution)/shard_map/ppermute | solution.py:587
  10.9 0.7 copy-start.1
  18.4 1.7 %collective-permute-start.2 = (bf16[336,384]{1,0:T(8,128)(2,1)}, bf16[336,384]{1,0:T(8,128)(2,1)S(1)}, u32[]{:S(2)}, u32[]{:S(2)}) collective-permute-start(bf16[336,384]{1,0:T(8,128)(2,1)} %get-tuple-element.42), channel_id=1, source_target_pairs={{0,16},{16,0},{1,17},{17,1},{2,18},{18,2},{3,19},{19,3},{4,20},{20... | collective-permute-start | bytes 774152 | tf_op jit(solution)/shard_map/ppermute | solution.py:587
  20.2 0.7 copy-start.3
  122.8 26.6 %copy-start.4 = (f32[8,384]{1,0:T(8,128)S(1)}, f32[8,384]{1,0:T(8,128)}, u32[]{:S(2)}) copy-start(f32[8,384]{1,0:T(8,128)} %get-tuple-element.61) | copy-start | bytes 36868
  122.8 28.4 %copy-start.2 = (f32[256,768]{1,0:T(8,128)S(1)}, f32[256,768]{1,0:T(8,128)}, u32[]{:S(2)}) copy-start(f32[256,768]{1,0:T(8,128)} %get-tuple-element.50) | copy-start | bytes 2359300
  147.6 4.4 %collective-permute-start.7 = (bf16[384,1536]{1,0:T(8,128)(2,1)}, bf16[384,1536]{1,0:T(8,128)(2,1)}, u32[]{:S(2)}, u32[]{:S(2)}) collective-permute-start(bf16[384,1536]{1,0:T(8,128)(2,1)} %get-tuple-element.59), channel_id=1, source_target_pairs={{0,16},{16,0},{1,17},{17,1},{2,18},{18,2},{3,19},{19,3},{4,20},{20... | collective-permute-start | bytes 3538952 | tf_op jit(solution)/shard_map/ppermute | solution.py:587
  147.6 3.6 %collective-permute-start.6 = (bf16[256,768]{1,0:T(8,128)(2,1)}, bf16[256,768]{1,0:T(8,128)(2,1)S(1)}, u32[]{:S(2)}, u32[]{:S(2)}) collective-permute-start(bf16[256,768]{1,0:T(8,128)(2,1)} %get-tuple-element.51), channel_id=1, source_target_pairs={{0,16},{16,0},{1,17},{17,1},{2,18},{18,2},{3,19},{19,3},{4,20},{20... | collective-permute-start | bytes 1179656 | tf_op jit(solution)/shard_map/ppermute | solution.py:587

commit v2 on v1

--- a/solution.py
+++ b/solution.py
@@ -57,7 +57,7 @@
 
 def attend_kernel(
     tm_ref, to_ref, wm_ref, wo_ref, vec_ref, hot_ref, msk_ref,
-    qkv_ref, keep_ref, send_ref, tr_ref, ctx_ref,
+    qkv_ref, keep_ref, send_ref, tr_ref, crow_ref, ctx_ref,
 ):
     s = lax.axis_index("seq")
     half, width = tm_ref.shape
@@ -98,6 +98,7 @@
     keep_ref[:half] = ctx_ref[:half]
     send_ref[:half] = ctx_ref[half:]
     keep_ref[half:] = rows
+    crow_ref[...] = rows
     send_ref[half:] = rows
 
 
@@ -172,75 +173,6 @@
     dctx_ref[...] = mm_nt(dat, wout_m[...]).astype(BF)
 
 
-def back_kernel(
-    qkv_ref, hot_ref, msk_ref, dctx_ref, tm_ref, to_ref, tr_ref, keep_ref, dat_ref, wm_ref, wo_ref,
-    dh1_ref, sums_ref,
-    load_ref, dkeep_ref, dsend_ref, small_ref,
-    dp_ref, part_ref,
-):
-    s = lax.axis_index("seq")
-    half, width = tm_ref.shape
-    own = width // 2
-    length = 2 * half
-    slots = dctx_ref.shape[0]
-    mine, other = lanes(s * own, own), lanes((1 - s) * own, own)
-    scale = HEAD_DIM**-0.5
-    hot = hot_ref[...]
-    valid = msk_ref[...] > 0.0
-    low = lax.broadcasted_iota(jnp.int32, (1, 128), 1) < HEAD_DIM
-    q_rows = (mm(hot, qkv_ref[:, :own]) * scale).astype(BF)
-    dq = []
-    for pair in range(own // 128):
-        at = pair * 128
-        keys = qkv_ref[:, own + at : own + at + 128]
-        vals = qkv_ref[:, 2 * own + at : 2 * own + at + 128]
-        q2, c2 = q_rows[:, at : at + 128], dctx_ref[:, at : at + 128]
-        zero = jnp.zeros_like(q2)
-        q4 = jnp.concatenate([jnp.where(low, q2, zero), jnp.where(low, zero, q2)], axis=0)
-        c4 = jnp.concatenate([jnp.where(low, c2, zero), jnp.where(low, zero, c2)], axis=0)
-        scores = jnp.where(valid, mm_nt(q4, keys), MASKED)
-        probs = jnp.exp(scores - jnp.max(scores, axis=-1, keepdims=True))
-        probs = probs / jnp.sum(probs, axis=-1, keepdims=True)
-        dprobs = mm_nt(c4, vals)
-        ds = probs * (dprobs - jnp.sum(probs * dprobs, axis=-1, keepdims=True))
-        ds = ds.astype(BF)
-        r = mm(ds, keys) * scale
-        dq.append(jnp.where(low, r[:slots], r[slots:]).astype(BF))
-        dp_ref[:, own + at : own + at + 128] = mm_tn(ds, q4).astype(BF)
-        dp_ref[:, 2 * own + at : 2 * own + at + 128] = mm_tn(probs.astype(BF), c4).astype(BF)
-    dq = jnp.concatenate(dq, axis=1)
-    dp_ref[:, :own] = mm_tn(hot, dq).astype(BF)
-    for side, cols in enumerate((other, mine)):
-        base = side * 3 * own
-        load_ref[base : base + own] = mm_tn(tr_ref[:, cols], dq).astype(BF)
-        for j in (1, 2):
-            g = mm_tn(tm_ref[:, cols], dp_ref[:half, j * own : (j + 1) * own])
-            g = g + mm_tn(to_ref[:, cols], dp_ref[half:, j * own : (j + 1) * own])
-            load_ref[base + j * own : base + (j + 1) * own] = g.astype(BF)
-    for h in range(2):
-        g = mm_tn(keep_ref[half:], dat_ref[:, h * own : (h + 1) * own])
-        load_ref[(6 + h) * own : (7 + h) * own] = g.astype(BF)
-    if load_ref.shape[0] > 8 * own:
-        load_ref[8 * own :] = jnp.zeros((load_ref.shape[0] - 8 * own, own), BF)
-    p_m = jnp.zeros((length, own), F32)
-    p_o = jnp.zeros((length, own), F32)
-    for j in range(3):
-        d = dp_ref[:, j * own : (j + 1) * own]
-        p_m = p_m + mm_nt(d, wm_ref[:, lanes(j * width + s * own, own)])
-        p_o = p_o + mm_nt(d, wo_ref[:, j * own : (j + 1) * own])
-    part_ref[:, mine] = p_m
-    part_ref[:, other] = p_o
-    dh1 = dh1_ref[...]
-    high = dh1.astype(BF)
-    rest = (dh1 - high.astype(F32)).astype(BF)
-    near = hot[:, :half]
-    dkeep_ref[...] = part_ref[:half] + mm_tn(near, high) + mm_tn(near, rest)
-    dsend_ref[...] = part_ref[half:].astype(BF)
-    small_ref[...] = sums_ref[:, mine]
-    small_ref[0:1] = jnp.sum(dq.astype(F32), axis=0, keepdims=True)
-    small_ref[1:2] = jnp.sum(dp_ref[:, 2 * own :].astype(F32), axis=0, keepdims=True)
-
-
 class Plan:
     def __init__(self, mesh, rows):
         axis = mesh.axis_names.index("batch")
@@ -299,20 +231,38 @@
 
 
 def reduce_kernel(
-    plan, load_ref, fac_ref, small_ref,
-    res_ref, got_ref, gath_ref, total_ref,
-    buf_ref, in_ref, sm_ref,
-    rs_send, rs_recv, ag_send, ag_recv, fa_send, fa_recv, fw_send, fw_recv, ow_send, ow_recv, sm_send, sm_recv, x_send, x_recv,
+    plan, fused,
+    fac_ref, qkv_ref, hot_ref, msk_ref, dctx_ref, tm_ref, to_ref, tr_ref, crow_ref, dat_ref, dh1_ref,
+    sums_ref, wqm_any, wqo_any, wum_any, wuo_any, wdm_any, upb_ref,
+    res_ref, got_ref, gath_ref, total_ref, dkeep_ref, drecv_ref, gdn_ref, gup_ref, gfar_ref, ubias_ref,
+    dbias_ref,
+    load_ref, buf_ref, in_ref, sm_ref, dp_ref, part_ref, dsend_ref, gnear_ref,
+    wqm_ref, wqo_ref, wum_ref, wuo_ref, wdm_ref,
+    rs_send, rs_recv, ag_send, ag_recv, fa_send, fa_recv, fw_send, fw_recv, ow_send, ow_recv,
+    sm_send, sm_recv, x_send, x_recv, d_send, d_recv, u_send, u_recv, w_sem,
 ):
     me = lax.axis_index("batch")
     s = lax.axis_index("seq")
     n, piece = plan.n, plan.piece
+    half, width = tm_ref.shape
+    own = width // 2
+    length = 2 * half
+    slots = dctx_ref.shape[0]
+    mine, other = lanes(s * own, own), lanes((1 - s) * own, own)
+    partner = {"seq": 1 - s}
+
+    fetched = [(wqm_any, wqm_ref), (wqo_any, wqo_ref)]
+    if fused:
+        fetched += [(wum_any, wum_ref), (wuo_any, wuo_ref), (wdm_any, wdm_ref)]
+    fetches = [pltpu.make_async_copy(a, b, w_sem.at[i]) for i, (a, b) in enumerate(fetched)]
+    for f in fetches:
+        f.start()
 
     barrier = pltpu.get_barrier_semaphore()
     for size, stride, o in plan.peers:
         to, _ = peer_of(me, size, stride, o)
         pl.semaphore_signal(barrier, inc=1, device_id={"batch": to}, device_id_type=MESH)
-    pl.semaphore_signal(barrier, inc=1, device_id={"seq": 1 - s}, device_id_type=MESH)
+    pl.semaphore_signal(barrier, inc=1, device_id=partner, device_id_type=MESH)
     pl.semaphore_wait(barrier, len(plan.peers) + 1)
 
     def copy(src, dst, send, recv, where):
@@ -468,37 +418,161 @@
 
     levels = len(plan.orders[0])
     last = levels - 1
-    running = {t: reduce_start(t, 0) for t in range(plan.streams)}
+    span = n * piece
     gathers = gather_stage(last)
     for h in range(2):
-        own_copy = copy(
-            window(h, ()), window(h, ()), ow_send.at[h], ow_recv.at[h], {"seq": 1 - s}
-        )
-        own_copy.start()
-        pending.append(own_copy.wait)
-    small = small_ref[...]
+        c = copy(window(h, ()), window(h, ()), ow_send.at[h], ow_recv.at[h], partner)
+        c.start()
+        pending.append(c.wait)
+
+    running = {}
+    ready = set()
+
+    def finished(first, end):
+        ready.update(range(first, end))
+        for t in range(plan.streams):
+            rows = [r for r in range(t * span, (t + 1) * span, own) if r < 8 * own]
+            if t not in running and all(r // own in ready for r in rows) and (
+                (min((t + 1) * span, 8 * own) - 1) // own in ready
+            ):
+                running[t] = reduce_start(t, 0)
+
+    if load_ref.shape[0] > 8 * own:
+        load_ref[8 * own :] = jnp.zeros((load_ref.shape[0] - 8 * own, own), BF)
+    for h in range(2):
+        g = mm_tn(crow_ref[...], dat_ref[:, h * own : (h + 1) * own])
+        load_ref[(6 + h) * own : (7 + h) * own] = g.astype(BF)
+    finished(6, 8)
+
+    scale = HEAD_DIM**-0.5
+    hot = hot_ref[...]
+    valid = msk_ref[...] > 0.0
+    low = lax.broadcasted_iota(jnp.int32, (1, 128), 1) < HEAD_DIM
+    q_rows = (mm(hot, qkv_ref[:, :own]) * scale).astype(BF)
+    dq = []
+    for pair in range(own // 128):
+        at = pair * 128
+        keys = qkv_ref[:, own + at : own + at + 128]
+        vals = qkv_ref[:, 2 * own + at : 2 * own + at + 128]
+        q2, c2 = q_rows[:, at : at + 128], dctx_ref[:, at : at + 128]
+        zero = jnp.zeros_like(q2)
+        q4 = jnp.concatenate([jnp.where(low, q2, zero), jnp.where(low, zero, q2)], axis=0)
+        c4 = jnp.concatenate([jnp.where(low, c2, zero), jnp.where(low, zero, c2)], axis=0)
+        scores = jnp.where(valid, mm_nt(q4, keys), MASKED)
+        probs = jnp.exp(scores - jnp.max(scores, axis=-1, keepdims=True))
+        probs = probs / jnp.sum(probs, axis=-1, keepdims=True)
+        dprobs = mm_nt(c4, vals)
+        ds = probs * (dprobs - jnp.sum(probs * dprobs, axis=-1, keepdims=True))
+        ds = ds.astype(BF)
+        r = mm(ds, keys) * scale
+        dq.append(jnp.where(low, r[:slots], r[slots:]).astype(BF))
+        dp_ref[:, own + at : own + at + 128] = mm_tn(ds, q4).astype(BF)
+        dp_ref[:, 2 * own + at : 2 * own + at + 128] = mm_tn(probs.astype(BF), c4).astype(BF)
+    dq = jnp.concatenate(dq, axis=1)
+    for side, cols in enumerate((other, mine)):
+        for j in range(3):
+            if j == 0:
+                g = mm_tn(tr_ref[:, cols], dq)
+            else:
+                g = mm_tn(tm_ref[:, cols], dp_ref[:half, j * own : (j + 1) * own])
+                g = g + mm_tn(to_ref[:, cols], dp_ref[half:, j * own : (j + 1) * own])
+            section = side * 3 + j
+            load_ref[section * own : (section + 1) * own] = g.astype(BF)
+            finished(section, section + 1)
+
+    dp_ref[:, :own] = mm_tn(hot, dq).astype(BF)
+    for f in fetches[:2]:
+        f.wait()
+    p_m = jnp.zeros((length, own), F32)
+    p_o = jnp.zeros((length, own), F32)
+    for j in range(3):
+        d = dp_ref[:, j * own : (j + 1) * own]
+        p_m = p_m + mm_nt(d, wqm_ref[:, lanes(j * width + s * own, own)])
+        p_o = p_o + mm_nt(d, wqo_ref[:, j * own : (j + 1) * own])
+    part_ref[:, mine] = p_m
+    part_ref[:, other] = p_o
+    dsend_ref[...] = part_ref[half:].astype(BF)
+    c = copy(dsend_ref, drecv_ref, d_send, d_recv, partner)
+    c.start()
+    pending.append(c.wait)
+    dh1 = dh1_ref[...]
+    high = dh1.astype(BF)
+    rest = (dh1 - high.astype(F32)).astype(BF)
+    near = hot[:, :half]
+    dkeep_ref[...] = part_ref[:half] + mm_tn(near, high) + mm_tn(near, rest)
+    small = sums_ref[:, mine]
+    row = lax.broadcasted_iota(jnp.int32, (8, 1), 0)
+    q_sum = jnp.sum(dq.astype(F32), axis=0, keepdims=True)
+    v_sum = jnp.sum(dp_ref[:, 2 * own :].astype(F32), axis=0, keepdims=True)
+    small = jnp.where(row == 0, q_sum, jnp.where(row == 1, v_sum, small))
+    gather_finish(gathers)
+    gathers = gather_stage(last - 1) if last >= 1 else []
+
+    chunks = []
+    if fused:
+        ff_own = wdm_ref.shape[0]
+        size = 256 if ff_own % 256 == 0 else ff_own
+        rows = n * slots
+
+        def factor(kind, h):
+            value = gath_ref[kind, h] if isinstance(h, int) else gath_ref[kind, pl.ds(h, 1)]
+            return value.reshape(rows, own)
+
+        def chunk(c):
+            cols = lanes(s * ff_own + c * size, size)
+            at = slice(c * size, (c + 1) * size)
+            near_x, far_x = factor(0, s), factor(0, 1 - s)
+            u = mm(near_x, wum_ref[:, cols]) + mm(far_x, wuo_ref[:, cols]) + upb_ref[:, cols]
+            phi = gelu_cdf(u)
+            g = (u * phi).astype(BF)
+            dg = mm_nt(factor(1, 0), wdm_ref[at, :own]) + mm_nt(factor(1, 1), wdm_ref[at, own:])
+            du = (dg * gelu_slope(u, phi)).astype(BF)
+            ubias_ref[:, at] = jnp.sum(du.astype(F32), axis=0, keepdims=True)
+            for h in range(2):
+                gdn_ref[at, h * own : (h + 1) * own] = mm_tn(g, factor(1, h)).astype(BF)
+            gup_ref[:, at] = mm_tn(near_x, du).astype(BF)
+            gnear_ref[:, at] = mm_tn(far_x, du).astype(BF)
+            x = copy(gnear_ref.at[:, at], gfar_ref.at[:, at], u_send.at[c], u_recv.at[c], partner)
+            x.start()
+            pending.append(x.wait)
+
+        chunks = list(range(ff_own // size))
+
+    cross = got_ref.shape[0]
+    small_ops = small_start(0, small)
     for level in range(levels):
-        small_ops = small_start(level, small)
-        gather_finish(gathers)
-        gathers = gather_stage(last - 1 - level) if level < last else []
+        if level > 0:
+            gather_finish(gathers)
+            gathers = gather_stage(last - 1 - level) if level < last else []
         for t in range(plan.streams):
             reduce_finish(t, level, running[t])
             running[t] = reduce_start(t, level + 1) if level < last else spread_start(t, last)
         small = small_finish(level, small_ops)
+        small_ops = small_start(level + 1, small) if level < last else []
     total_ref[...] = small
-    cross = got_ref.shape[0]
-    span = n * piece
+    for wait in pending:
+        wait()
+    pending.clear()
+    if fused:
+        for f in fetches[2:]:
+            f.wait()
+        for h in range(2):
+            dbias_ref[h : h + 1] = jnp.sum(factor(1, h).astype(F32), axis=0, keepdims=True)
     for level in range(last, -1, -1):
         for t in range(plan.streams):
+            if chunks and t % 2 == 0:
+                chunk(chunks.pop(0))
             for c in running[t]:
                 c.wait()
             if level > 0:
                 running[t] = spread_start(t, level - 1)
             elif t * span < cross:
-                rows = pl.ds(t * span, min(span, cross - t * span))
-                x = copy(res_ref.at[rows], got_ref.at[rows], x_send.at[t], x_recv.at[t], {"seq": 1 - s})
+                rows_x = pl.ds(t * span, min(span, cross - t * span))
+                x = copy(res_ref.at[rows_x], got_ref.at[rows_x], x_send.at[t], x_recv.at[t], partner)
                 x.start()
                 pending.append(x.wait)
+    while chunks:
+        chunk(chunks.pop(0))
     for wait in pending:
         wait()
 
@@ -506,7 +580,7 @@
 def ffn_kernel(
     gath_ref, wup_m, wup_o, wdn_m, upb_ref,
     gdn_ref, gup_ref, gsend_ref, bias_ref, dbias_ref,
-    far_ref,
+    down_ref, near_ref, far_ref,
 ):
     s = lax.axis_index("seq")
     step, steps = pl.program_id(0), pl.num_programs(0)
@@ -517,7 +591,7 @@
 
     @pl.when(step == 0)
     def _():
-        for ref in (gdn_ref, gup_ref, far_ref, bias_ref, dbias_ref):
+        for ref in (down_ref, near_ref, far_ref, bias_ref, dbias_ref):
             ref[...] = jnp.zeros_like(ref)
 
     for h in range(2):
@@ -533,26 +607,33 @@
         du = (dg * gelu_slope(u, phi)).astype(BF)
         bias_ref[:, at] += jnp.sum(du.astype(F32), axis=0, keepdims=True)
         for h in range(2):
-            gdn_ref[at, h * own : (h + 1) * own] += mm_tn(g, gath_ref[1, h])
-        gup_ref[:, at] += mm_tn(gath_ref[0, sides[0]][0], du)
+            down_ref[at, h * own : (h + 1) * own] += mm_tn(g, gath_ref[1, h])
+        near_ref[:, at] += mm_tn(gath_ref[0, sides[0]][0], du)
         far_ref[:, at] += mm_tn(gath_ref[0, sides[1]][0], du)
 
     @pl.when(step == steps - 1)
     def _():
         gsend_ref[...] = far_ref[...].astype(BF)
-
-
-def final_kernel(res_ref, got_ref, gup_ref, grecv_ref, gqkv_out, gout_out, gup_out):
+        gdn_ref[...] = down_ref[...].astype(BF)
+        gup_ref[...] = near_ref[...].astype(BF)
+
+
+def final_kernel(
+    own_ref, out_ref, got_ref, gup_ref, gfar_ref, gdn_ref, dkeep_ref, drecv_ref,
+    gqkv_out, gout_out, gup_out, gdn_out, gtok_out,
+):
     s = lax.axis_index("seq")
-    own = gout_out.shape[0]
+    own = got_ref.shape[2]
     width, ff_own = 2 * own, gup_ref.shape[1]
     for j in range(3):
-        gqkv_out[:, lanes(j * width + s * own, own)] = res_ref[(3 + j) * own : (4 + j) * own].astype(F32)
-        gqkv_out[:, lanes(j * width + (1 - s) * own, own)] = got_ref[j * own : (j + 1) * own].astype(F32)
+        gqkv_out[:, lanes(j * width + s * own, own)] = own_ref[j].astype(F32)
+        gqkv_out[:, lanes(j * width + (1 - s) * own, own)] = got_ref[j].astype(F32)
     for h in range(2):
-        gout_out[:, h * own : (h + 1) * own] = res_ref[(6 + h) * own : (7 + h) * own].astype(F32)
-    gup_out[:, lanes(s * ff_own, ff_own)] = gup_ref[...]
-    gup_out[:, lanes((1 - s) * ff_own, ff_own)] = grecv_ref[...].astype(F32)
+        gout_out[:, h * own : (h + 1) * own] = out_ref[h].astype(F32)
+    gup_out[:, lanes(s * ff_own, ff_own)] = gup_ref[...].astype(F32)
+    gup_out[:, lanes((1 - s) * ff_own, ff_own)] = gfar_ref[...].astype(F32)
+    gdn_out[...] = gdn_ref[...].astype(F32)
+    gtok_out[...] = (dkeep_ref[...] + drecv_ref[...].astype(F32)).astype(BF)
 
 
 def shape(dims, kind=BF):
@@ -601,10 +682,10 @@
     hot = ((grad_pos[0][:, None] == pos[None, :]) & live).astype(BF)
     msk = (pos < seq_len[0]).astype(F32)[None]
 
-    qkv, keep, send, tr = local_call(
+    qkv, keep, send, tr, crow = local_call(
         attend_kernel,
         [shape((length, 3 * own)), shape((half + slots, own)), shape((half + slots, own)),
-         shape((slots, width))],
+         shape((slots, width)), shape((slots, own))],
         [pltpu.VMEM((length, own), BF)],
     )(tm, to, w_qkv, wqkv_o, vec, hot, msk)
     recv = swap(send)
@@ -617,26 +698,29 @@
          pltpu.VMEM((slots, width), F32)],
         scalars=1, args=14,
     )(grad_count, keep, recv, tm, tr, w_out, wout_o, w_up, wup_o, w_down, wdn_o, vec, upb, out_grad[0])
-    load, dkeep, dsend, small = local_call(
-        back_kernel,
-        [shape((plan.rows, own)), shape((half, width), F32), shape((half, width)),
-         shape((8, own), F32)],
-        [pltpu.VMEM((length, 3 * own), BF), pltpu.VMEM((length, width), F32)],
-    )(qkv, hot, msk, dctx, tm, to, tr, keep, dat, w_qkv, wqkv_o, dh1, sums)
-    drecv = swap(dsend)
-    grad_tok = (dkeep + drecv.astype(F32)).astype(BF)[None]
-
     dma = pltpu.SemaphoreType.DMA
     depth, widest = len(plan.orders[0]), max(size for size, _ in plan.orders[0]) - 1
     slots_small = sum(size for size, _ in plan.orders[0])
-    cross = 3 * own
-    res, got, gath, total = pl.pallas_call(
-        functools.partial(reduce_kernel, plan),
-        out_shape=[shape((plan.rows, own)), shape((cross, own)), shape((2, 2, *(size for size, _ in plan.orders[0]), slots, own)),
-                   shape((8, own), F32)],
+    cross, rows = 3 * own, n * slots
+    fused = rows <= 1280
+    sizes = tuple(size for size, _ in plan.orders[0])
+    keep_ff = (lambda *dims: dims) if fused else (lambda *dims: (16, 128))
+    vmem, hbm = pl.BlockSpec(memory_space=pltpu.VMEM), pl.BlockSpec(memory_space=pl.ANY)
+    res, got, gath, total, dkeep, drecv, gdn, gup, gfar, ubias, dbias = pl.pallas_call(
+        functools.partial(reduce_kernel, plan, fused),
+        in_specs=[vmem] * 12 + [hbm] * 5 + [vmem],
+        out_shape=[shape((plan.rows, own)), shape((cross, own)), shape((2, 2, *sizes, slots, own)),
+                   shape((8, own), F32), shape((half, width), F32), shape((half, width)),
+                   shape(keep_ff(ff_own, width)), shape(keep_ff(own, ff_own)),
+                   shape(keep_ff(own, ff_own)), shape((1, ff_own), F32), shape((2, own), F32)],
         scratch_shapes=[
             pltpu.VMEM((plan.rows, own), BF), pltpu.VMEM((plan.rows, own), BF),
-            pltpu.VMEM((slots_small, 8, own), F32),
+            pltpu.VMEM((plan.rows, own), BF), pltpu.VMEM((slots_small, 8, own), F32),
+            pltpu.VMEM((length, 3 * own), BF), pltpu.VMEM((length, width), F32),
+            pltpu.VMEM((half, width), BF), pltpu.VMEM(keep_ff(own, ff_own), BF),
+            pltpu.VMEM((own, 3 * width), BF), pltpu.VMEM((own, 3 * own), BF),
+            pltpu.VMEM(keep_ff(own, ff), BF), pltpu.VMEM(keep_ff(own, ff), BF),
+            pltpu.VMEM(keep_ff(ff_own, width), BF),
             dma((plan.streams, plan.copies)), dma((plan.streams, plan.copies)),
             dma((plan.streams, plan.copies)), dma((plan.streams, plan.copies)),
             dma((2, depth, widest)), dma((2, depth, widest)),
@@ -644,34 +728,50 @@
             dma((2,)), dma((2,)),
             dma((slots_small,)), dma((slots_small,)),
             dma((plan.streams,)), dma((plan.streams,)),
+            dma, dma, dma((8,)), dma((8,)), dma((5,)),
         ],
         compiler_params=pltpu.CompilerParams(
             collective_id=0, has_side_effects=True, vmem_limit_bytes=VMEM_LIMIT
         ),
-    )(load, fac, small)
-
-    rows = n * slots
-    tile = rows if rows <= 1280 else 1280 if rows % 1280 == 0 else slots
-    fixed = lambda *dims: pl.BlockSpec(dims, lambda i: (0,) * len(dims), pipeline_mode=pl.Buffered(1))
-    gdn, gup, gsend, ubias, dbias = pl.pallas_call(
-        ffn_kernel,
-        grid=(rows // tile,),
-        in_specs=[pl.BlockSpec((2, 2, tile, own), lambda i: (0, 0, i, 0)), fixed(own, ff),
-                  fixed(own, ff), fixed(ff_own, width), fixed(1, ff)],
-        out_specs=[fixed(ff_own, width), fixed(own, ff_own), fixed(own, ff_own), fixed(1, ff_own),
-                   fixed(2, own)],
-        out_shape=[shape((ff_own, width), F32), shape((own, ff_own), F32), shape((own, ff_own)),
-                   shape((1, ff_own), F32), shape((2, own), F32)],
-        scratch_shapes=[pltpu.VMEM((own, ff_own), F32)],
+    )(fac, qkv, hot, msk, dctx, tm, to, tr, crow, dat, dh1, sums, w_qkv, wqkv_o, w_up, wup_o, w_down, upb)
+
+    if not fused:
+        tile = 1280 if rows % 1280 == 0 else slots
+        fixed = lambda *dims: pl.BlockSpec(dims, lambda i: (0,) * len(dims), pipeline_mode=pl.Buffered(1))
+        gdn, gup, gsend, ubias, dbias = pl.pallas_call(
+            ffn_kernel,
+            grid=(rows // tile,),
+            in_specs=[pl.BlockSpec((2, 2, tile, own), lambda i: (0, 0, i, 0)), fixed(own, ff),
+                      fixed(own, ff), fixed(ff_own, width), fixed(1, ff)],
+            out_specs=[fixed(ff_own, width), fixed(own, ff_own), fixed(own, ff_own),
+                       fixed(1, ff_own), fixed(2, own)],
+            out_shape=[shape((ff_own, width)), shape((own, ff_own)), shape((own, ff_own)),
+                       shape((1, ff_own), F32), shape((2, own), F32)],
+            scratch_shapes=[pltpu.VMEM((ff_own, width), F32), pltpu.VMEM((own, ff_own), F32),
+                            pltpu.VMEM((own, ff_own), F32)],
+            compiler_params=pltpu.CompilerParams(vmem_limit_bytes=VMEM_LIMIT),
+        )(gath.reshape(2, 2, rows, own), w_up, wup_o, w_down, upb)
+        gfar = swap(gsend)
+    cut = 4 if own % 64 == 0 else 1
+    block = own // cut
+    res = res[: 8 * own].reshape(8, own, own)
+    flat = lambda r, c: pl.BlockSpec((r, c), lambda i: (i, 0))
+    gqkv, gout, gup, gdn, gtok = pl.pallas_call(
+        final_kernel,
+        grid=(cut,),
+        in_specs=[pl.BlockSpec((3, block, own), lambda i: (1, i, 0)),
+                  pl.BlockSpec((2, block, own), lambda i: (3, i, 0)),
+                  pl.BlockSpec((3, block, own), lambda i: (0, i, 0)),
+                  flat(block, ff_own), flat(block, ff_own), flat(ff_own // cut, width),
+                  flat(half // cut, width), flat(half // cut, width)],
+        out_specs=[flat(block, 3 * width), flat(block, width), flat(block, ff),
+                   flat(ff_own // cut, width), flat(half // cut, width)],
+        out_shape=[shape((own, 3 * width), F32), shape((own, width), F32), shape((own, ff), F32),
+                   shape((ff_own, width), F32), shape((half, width))],
         compiler_params=pltpu.CompilerParams(vmem_limit_bytes=VMEM_LIMIT),
-    )(gath.reshape(2, 2, rows, own), w_up, wup_o, w_down, upb)
-    grecv = swap(gsend)
-    gqkv, gout, gup = local_call(
-        final_kernel,
-        [shape((own, 3 * width), F32), shape((own, width), F32), shape((own, ff), F32)],
-    )(res, got, gup, grecv)
+    )(res, res, got.reshape(3, own, own), gup, gfar, gdn, dkeep, drecv)
     return (
-        out[None], grad_tok, gqkv, total[0], total[1], gout, total[2], total[3], total[4], gup,
+        out[None], gtok[None], gqkv, total[0], total[1], gout, total[2], total[3], total[4], gup,
         ubias[0], gdn, lax.dynamic_index_in_dim(dbias, s, 0, keepdims=False), total[5], total[6],
     )
 

time: 160 us -> 131 us (0.82)
  Pallas kernels: 141 us -> 114 us
    pallas_call x4 -> x2, Pallas kernels: 120 us -> 92.9 us  [the longest x1 83.8 us: body(): pl.pallas_call(functools.partial(reduce_kernel, plan, fused), in_specs=[v...]
    ppermute x8 -> x6, waiting for transfers between devices: 5.54 us -> 4.94 us  [body(): swap = lambda x: lax.ppermute(x, 'seq', [(0, 1), (1, 0)])]
  transfers between devices with their start and end apart: 8 -> 6, of which waited for: 3 -> 2; matrix products, arithmetic and copies ran while one was open for 4% -> 3% of each run, Pallas kernels for 4% -> 5%
where the time goes in v2:
time: 131 us
  Pallas kernels  114 us (87%)
  local copies, waits for them, and re-layouts  5.06 us (4%)
  waiting for transfers between devices  4.94 us (4%)
  other arithmetic  2.71 us (2%)
  between operations  2.34 us (2%)
  starting transfers between devices  2.02 us (2%)
    pallas_call x1, Pallas kernels, body(): pl.pallas_call(functools.partial(reduce_kernel, plan, fused), in_specs=[v...  83.8 us
    pallas_call x1, Pallas kernels, body(): local_call(feed_kernel, [shape((half, width)), shape((2, 2, slots, own)),...  14.2 us
    pallas_call x1, Pallas kernels, body(): pl.pallas_call(final_kernel, grid=(cut,), in_specs=[pl.BlockSpec((3, bloc...  9.13 us
    pallas_call x1, Pallas kernels, body(): local_call(attend_kernel, [shape((length, 3 * own)), shape((half + slots,...  6.83 us
    ppermute x6, waiting for transfers between devices, body(): swap = lambda x: lax.ppermute(x, 'seq', [(0, 1), (1, 0)])  4.94 us
  transfers between devices with their start and end apart: 6, of which 2 were waited for; matrix products, arithmetic and copies ran while one was open for 3% of the time, Pallas kernels for 5%

profile of v2, /device:TPU:0, one launch (start us, length us, event | category | flops | bytes accessed | tf_op | source)
XLA Modules:
  0.0 131.1 jit_solution(1335158234796502047)
XLA Ops:
  0.7 0.6 collective-permute-start.4
  1.2 0.1 collective-permute-start.5
  1.3 0.0 copy-start
  1.3 0.0 copy-start.3
  1.3 0.0 copy-start.4
  1.3 0.0 copy-start.5
  1.3 0.0 copy-start.6
  1.3 0.0 copy-start.7
  1.3 0.0 copy-start.8
  1.3 0.0 copy-start.9
  1.3 0.0 copy-start.10
  1.4 0.0 copy-start.11
  1.4 1.3 constant_dynamic-slice_fusion.2
  2.7 0.1 pad_maximum_fusion
  2.8 0.5 collective-permute-start.1
  3.3 0.0 copy-done
  3.3 0.1 collective-permute-start
  3.3 0.4 collective-permute-start.3
  4.4 0.6 compare_convert_fusion.msk_ref
  5.7 0.0 copy-done.3
  5.7 0.0 copy-done.4
  5.7 0.0 copy-done.5
  5.7 0.0 copy-done.6
  5.8 0.0 copy-done.7
  5.8 0.0 copy-done.8
  5.8 0.0 copy-done.9
  5.8 0.0 copy-done.10
  5.9 0.6 stack.35.vec_ref
  6.5 0.0 copy-done.11
  6.5 0.7 and_convert_fusion.hot_ref
  7.2 3.6 %collective-permute-done.to_ref = bf16[256,768]{1,0:T(8,128)(2,1)S(1)} collective-permute-done((bf16[256,768]{1,0:T(8,128)(2,1)S(1)}, bf16[256,768]{1,0:T(8,128)(2,1)S(1)}, u32[]{:S(2)}, u32[]{:S(2)}) %collective-permute-start) | collective-permute-done | bytes 393248 | tf_op jit(solution)/shard_map/ppermute | solution.py:668
  10.8 0.0 copy-start.1
  10.8 0.0 collective-permute-done.1.wo_ref.wqo_any
  10.8 0.7 copy-done.1
  11.5 6.8 %shard_map.289 = (bf16[512,1152]{1,0:T(8,128)(2,1)}, bf16[336,384]{1,0:T(8,128)(2,1)}, bf16[336,384]{1,0:T(8,128)(2,1)}, bf16[80,768]{1,0:T(8,128)(2,1)}, bf16[80,384]{1,0:T(8,128)(2,1)}) custom-call(bf16[256,768]{1,0:T(8,128)(2,1)} %bitcast.14, bf16[256,768]{1,0:T(8,128)(2,1)} %copy-done.1, bf16[384,2304]{1,0:T(8,128)(2,1)} %wqm_any.1, ...), custom_call_target="tpu_custom_call" | custom-call | tf_op jit(solution)/shard_map/pallas_call | solution.py:685
  18.4 0.4 collective-permute-start.2
  18.7 0.0 collective-permute-done.3.wout_o
  18.7 1.4 %collective-permute-done.2.recv_ref = bf16[336,384]{1,0:T(8,128)(2,1)S(1)} collective-permute-done((bf16[336,384]{1,0:T(8,128)(2,1)}, bf16[336,384]{1,0:T(8,128)(2,1)S(1)}, u32[]{:S(2)}, u32[]{:S(2)}) %collective-permute-start.2) | collective-permute-done | bytes 258080 | tf_op jit(solution)/shard_map/ppermute | solution.py:668
  20.1 0.0 copy-start.2
  20.1 0.0 collective-permute-done.4.wup_o.wuo_any
  20.1 0.0 collective-permute-done.5.wdn_o
  20.1 0.7 copy-done.2
  20.8 14.2 %shard_map.290 = (bf16[256,768]{1,0:T(8,128)(2,1)}, bf16[2,2,80,384]{3,2,1,0:T(8,128)(2,1)}, bf16[80,768]{1,0:T(8,128)(2,1)}, f32[80,768]{1,0:T(8,128)}, bf16[80,384]{1,0:T(8,128)(2,1)}, /*index=5*/f32[8,768]{1,0:T(8,128)}) custom-call(s32[1]{0:T(128)} %copy.34.count_ref, bf16[336,384]{1,0:T(8,128)(2,1)} %get-tuple-element.41.keep_ref, ...), custom_call_target="tpu_custom_call" | custom-call | tf_op jit(solution)/shard_map/pallas_call | solution.py:692
  35.0 83.8 %shard_map.291 = (bf16[3072,384]{1,0:T(8,128)(2,1)}, bf16[1152,384]{1,0:T(8,128)(2,1)}, bf16[2,2,2,2,4,80,384]{6,5,4,3,2,1,0:T(8,128)(2,1)}, f32[8,384]{1,0:T(8,...) custom-call(bf16[2,2,80,384]{3,2,1,0:T(8,128)(2,1)} %get-tuple-eleme, ...), custom_call_target="tpu_custom_call" | custom-call | tf_op jit(solution)/shard_map/pallas_call | solution.py:709
  118.9 1.3 %reduce.5 = f32[1536]{0:T(1024)} reduce(f32[1,1536]{1,0:T(1,128)} %get-tuple-element.64, f32[]{:T(128)} %constant.37), dimensions={0}, to_apply=%get-tuple-element.64.reduce_sub_computation | reduce | bytes 12292 | tf_op jit(solution)/shard_map/pallas_call | solution.py:709
  120.2 1.6 %slice_reduce_fusion = (f32[384]{0:T(512)}, f32[384]{0:T(512)}, f32[384]{0:T(512)}, f32[384]{0:T(512)}, f32[384]{0:T(512)}, /*index=5*/f32[384]{0:T(512)}, f32[384]{0:T(512)}, f32[384]{0:T(512)}) fusion(f32[8,384]{1,0:T(8,128)} %get-tuple-element.61, f32[2,384]{1,0:T(2,128)} %get-tuple-element.66, s32[]{:T(128)S(6)} %select_n.34), kind=kLoop, calls=%fused_computation.6 | loop fusion | bytes 24580 | tf_op jit(solution)/shard_map/slice | solution.py:775
  121.8 9.1 %shard_map.292 = (f32[384,2304]{1,0:T(8,128)}, f32[384,768]{1,0:T(8,128)}, f32[384,3072]{1,0:T(8,128)}, f32[1536,768]{1,0:T(8,128)}, bf16[256,768]{1,0:T(8,128)(2,1)}) custom-call(bf16[8,384,384]{2,1,0:T(8,128)(2,1)} %bitcast.12, bf16[8,384,384]{2,1,0:T(8,128)(2,1)} %bitcast.13, bf16[3,384,384]{2,1,0:T(8,128)(2,1)} %bitcast.18, ...), custom_call_target="tpu_custom_call" | custom-call | tf_op jit(solution)/shard_map/pallas_call | solution.py:759
  (10 shorter events, 0.0 us)
Async XLA Ops:
  0.7 19.5 %collective-permute-start.4 = (bf16[384,3072]{1,0:T(8,128)(2,1)}, bf16[384,3072]{1,0:T(8,128)(2,1)}, u32[]{:S(2)}, u32[]{:S(2)}) collective-permute-start(bf16[384,3072]{1,0:T(8,128)(2,1)} %wum_any.1), channel_id=1, source_target_pairs={{0,16},{16,0},{1,17},{17,1},{2,18},{18,2},{3,19},{19,3},{4,20},{20... | collective-permute-start | bytes 7077896 | tf_op jit(solution)/shard_map/ppermute | solution.py:668
  1.2 18.9 %collective-permute-start.5 = (bf16[1536,768]{1,0:T(8,128)(2,1)}, bf16[1536,768]{1,0:T(8,128)(2,1)}, u32[]{:S(2)}, u32[]{:S(2)}) collective-permute-start(bf16[1536,768]{1,0:T(8,128)(2,1)} %wdm_any.1), channel_id=1, source_target_pairs={{0,16},{16,0},{1,17},{17,1},{2,18},{18,2},{3,19},{19,3},{4,20},{20... | collective-permute-start | bytes 7077896 | tf_op jit(solution)/shard_map/ppermute | solution.py:668
  1.3 2.0 %copy-start = (bf16[1,256,768]{2,1,0:T(8,128)(2,1)S(1)}, bf16[1,256,768]{2,1,0:T(8,128)(2,1)}, u32[]{:S(2)}) copy-start(bf16[1,256,768]{2,1,0:T(8,128)(2,1)} %param.18) | copy-start | bytes 1179652
  1.3 4.4 %copy-start.3 = (f32[768]{0:T(1024)S(1)}, f32[768]{0:T(1024)}, u32[]{:S(2)}) copy-start(f32[768]{0:T(1024)} %param.23) | copy-start | bytes 9220
  1.3 4.4 %copy-start.4 = (f32[768]{0:T(1024)S(1)}, f32[768]{0:T(1024)}, u32[]{:S(2)}) copy-start(f32[768]{0:T(1024)} %param.24) | copy-start | bytes 9220
  1.3 4.4 %copy-start.5 = (f32[768]{0:T(1024)S(1)}, f32[768]{0:T(1024)}, u32[]{:S(2)}) copy-start(f32[768]{0:T(1024)} %param.25) | copy-start | bytes 9220
  1.3 4.4 %copy-start.6 = (f32[768]{0:T(1024)S(1)}, f32[768]{0:T(1024)}, u32[]{:S(2)}) copy-start(f32[768]{0:T(1024)} %param.29) | copy-start | bytes 9220
  1.3 4.5 %copy-start.7 = (f32[768]{0:T(1024)S(1)}, f32[768]{0:T(1024)}, u32[]{:S(2)}) copy-start(f32[768]{0:T(1024)} %param.30) | copy-start | bytes 9220
  1.3 4.5 %copy-start.8 = (f32[768]{0:T(1024)S(1)}, f32[768]{0:T(1024)}, u32[]{:S(2)}) copy-start(f32[768]{0:T(1024)} %param.31) | copy-start | bytes 9220
  1.3 4.5 %copy-start.9 = (f32[768]{0:T(1024)S(1)}, f32[768]{0:T(1024)}, u32[]{:S(2)}) copy-start(f32[768]{0:T(1024)} %param.20) | copy-start | bytes 9220
  1.3 4.5 %copy-start.10 = (f32[768]{0:T(1024)S(1)}, f32[768]{0:T(1024)}, u32[]{:S(2)}) copy-start(f32[768]{0:T(1024)} %param.21) | copy-start | bytes 9220
  1.4 5.1 %copy-start.11 = (s32[1,80]{1,0:T(1,128)S(1)}, s32[1,80]{1,0:T(1,128)}, u32[]{:S(2)}) copy-start(s32[1,80]{1,0:T(1,128)} %param.33) | copy-start | bytes 964
  2.8 8.0 %collective-permute-start.1 = (bf16[384,1152]{1,0:T(8,128)(2,1)S(1)}, bf16[384,1152]{1,0:T(8,128)(2,1)}, u32[]{:S(2)}, u32[]{:S(2)}) collective-permute-start(bf16[384,1152]{1,0:T(8,128)(2,1)S(1)} %pad_maximum_fusion), channel_id=1, source_target_pairs={{0,16},{16,0},{1,17},{17,1},{2,18},{18,2},{3,19},{19,3},{4,20},{20... | collective-permute-start | bytes 2654216 | tf_op jit(solution)/shard_map/ppermute | solution.py:668
  3.3 7.5 %collective-permute-start = (bf16[256,768]{1,0:T(8,128)(2,1)S(1)}, bf16[256,768]{1,0:T(8,128)(2,1)S(1)}, u32[]{:S(2)}, u32[]{:S(2)}) collective-permute-start(bf16[256,768]{1,0:T(8,128)(2,1)S(1)} %bitcast.17), channel_id=1, source_target_pairs={{0,16},{16,0},{1,17},{17,1},{2,18},{18,2},{3,19},{19,3},{4,20},{20... | collective-permute-start | bytes 1179656 | tf_op jit(solution)/shard_map/ppermute | solution.py:668
  3.3 15.4 %collective-permute-start.3 = (bf16[384,768]{1,0:T(8,128)(2,1)}, bf16[384,768]{1,0:T(8,128)(2,1)}, u32[]{:S(2)}, u32[]{:S(2)}) collective-permute-start(bf16[384,768]{1,0:T(8,128)(2,1)} %wout_m.1), channel_id=1, source_target_pairs={{0,16},{16,0},{1,17},{17,1},{2,18},{18,2},{3,19},{19,3},{4,20},{20... | collective-permute-start | bytes 1769480 | tf_op jit(solution)/shard_map/ppermute | solution.py:668
  10.8 0.7 copy-start.1
  18.4 1.7 %collective-permute-start.2 = (bf16[336,384]{1,0:T(8,128)(2,1)}, bf16[336,384]{1,0:T(8,128)(2,1)S(1)}, u32[]{:S(2)}, u32[]{:S(2)}) collective-permute-start(bf16[336,384]{1,0:T(8,128)(2,1)} %get-tuple-element.42), channel_id=1, source_target_pairs={{0,16},{16,0},{1,17},{17,1},{2,18},{18,2},{3,19},{19,3},{4,20},{20... | collective-permute-start | bytes 774152 | tf_op jit(solution)/shard_map/ppermute | solution.py:668
  20.1 0.7 copy-start.2

commit v3 on v2

v3 whole, which is shorter than its diff:
```python
import functools
import math

import jax
import jax.numpy as jnp
import numpy as np
from jax import lax
from jax.experimental import pallas as pl
from jax.experimental.pallas import tpu as pltpu
from jax.sharding import PartitionSpec as P

HEAD_DIM = 64
NORM_EPS = 1e-05
MASKED = -1000000000.0
BF = jnp.bfloat16
F32 = jnp.float32
MESH = pl.DeviceIdType.MESH
VMEM_LIMIT = 63 * 1024 * 1024


def mm(a, b):
    return lax.dot_general(a, b, (((1,), (0,)), ((), ())), preferred_element_type=F32)


def mm_nt(a, b):
    return lax.dot_general(a, b, (((1,), (1,)), ((), ())), preferred_element_type=F32)


def mm_tn(a, b):
    return lax.dot_general(a, b, (((0,), (0,)), ((), ())), preferred_element_type=F32)


def lanes(start, size):
    return pl.ds(pl.multiple_of(start, 128), size)


def gelu_cdf(u):
    return 0.5 + 0.5 * lax.erf(u * (2.0**-0.5))


def gelu_slope(u, phi):
    return phi + u * ((2.0 * math.pi) ** -0.5) * jnp.exp(-0.5 * u * u)


def norm_stats(x):
    center = x - jnp.mean(x, axis=-1, keepdims=True)
    inverse = lax.rsqrt(jnp.mean(center * center, axis=-1, keepdims=True) + NORM_EPS)
    return center * inverse, inverse


def norm_back(up, unit, inverse, gain):
    e = up * gain
    return inverse * (
        e - jnp.mean(e, axis=-1, keepdims=True) - unit * jnp.mean(e * unit, axis=-1, keepdims=True)
    )


def pick(value, which, own):
    return jnp.where(which == 0, value[:, :own], value[:, own:])


class Plan:
    def __init__(self, mesh, rows):
        axis = mesh.axis_names.index("batch")
        line = np.moveaxis(mesh.devices, axis, 0)
        line = line.reshape(line.shape[0], -1)[:, 0]
        n = len(line)
        self.n = n
        dims = []
        try:
            coords = [tuple(d.coords) for d in line]
            for d in range(3):
                size = len({c[d] for c in coords})
                if size > 1:
                    first = coords[0]
                    stride = next(
                        i
                        for i, c in enumerate(coords)
                        if c[d] != first[d] and all(c[e] == first[e] for e in range(3) if e != d)
                    )
                    dims.append((size, stride))
            good = all(
                c[d] >= 0 for c in coords for d in range(3)
            ) and math.prod(size for size, _ in dims) == n
            if not good:
                dims = []
        except (AttributeError, StopIteration):
            dims = []
        if not dims:
            rest, stride = n, 1
            while rest > 1:
                dims.append((2 if rest % 2 == 0 else rest, stride))
                stride *= dims[-1][0]
                rest //= dims[-1][0]
        dims.sort()
        self.orders = [dims]
        if len(dims) > 1:
            self.orders.append([dims[1], dims[0]] + dims[2:])
        halves = []
        for size, stride in dims:
            if size > 2 and size & (size - 1) == 0:
                while size > 1:
                    halves.append((2, stride))
                    size, stride = size // 2, stride * 2
            else:
                halves.append((size, stride))
        first = 2 if len(dims) > 1 and dims[0][0] == dims[1][0] == 2 else 0
        plain = halves
        turned = [halves[1], halves[0]] + halves[2:] if first else halves
        deep = halves[2:] + [halves[1], halves[0]] if first and len(halves) > 3 else plain
        self.lanes = [plain, turned, plain, deep]
        self.peers = [(size, stride, o) for size, stride in dims for o in range(1, size)]
        unit = 16 * n
        streams = max(2, min(4, rows // unit))
        streams += streams % 2
        self.piece = -(-rows // (streams * unit)) * 16
        self.streams = streams
        self.rows = streams * n * self.piece
        self.copies = sum(size - 1 for size, _ in halves)


def coordinate(me, size, stride):
    return lax.rem(lax.div(me, stride), size)


def peer_of(me, size, stride, offset):
    here = coordinate(me, size, stride)
    there = lax.rem(here + offset, size)
    return me + (there - here) * stride, there


def layer_kernel(
    plan, fused,
    len_ref, count_ref, tm_ref, gp_ref, grad_ref, ob_ref, g1_ref, s1_ref, db_ref, g2_ref, s2_ref, qb_ref,
    vb_ref, upb_ref, wq_any, wo_any, wu_any, wd_any,
    out_out, res_out, got_out, total_ref, dkeep_out, drecv_out, gdn_out, gup_out, gfar_out,
    ubias_ref, dbias_ref, gath_ref, wuo_ref,
    out_ref, res_ref, dkeep_ref, gdn_ref, gup_ref,
    to_ref, wqm_ref, wqo_ref, wom_ref, woo_ref, wum_ref, wdm_ref, wdo_ref, qkv_ref, ctx_ref, crow_ref,
    crecv_ref, ab_ref, acc_ref, slope_ref, da_ref, load_ref, buf_ref, in_ref, sm_ref, dp_ref, part_ref,
    dsend_ref, gnear_ref, fac_ref,
    rs_send, rs_recv, ag_send, ag_recv, fa_send, fa_recv, fw_send, fw_recv, ow_send, ow_recv,
    sm_send, sm_recv, x_send, x_recv, d_send, d_recv, u_send, u_recv, c_send, c_recv, w_send, w_recv, w_sem, o_sem,
):
    me = lax.axis_index("batch")
    s = lax.axis_index("seq")
    n, piece = plan.n, plan.piece
    half, width = tm_ref.shape
    own = width // 2
    length = 2 * half
    slots = grad_ref.shape[0]
    ff_own = wdm_ref.shape[0]
    mine, other = lanes(s * own, own), lanes((1 - s) * own, own)
    partner = {"seq": 1 - s}

    fetches = [
        pltpu.make_async_copy(a, b, w_sem.at[i])
        for i, (a, b) in enumerate(
            [(wq_any, wqm_ref), (wo_any, wom_ref), (wu_any, wum_ref), (wd_any, wdm_ref)]
        )
    ]
    for f in fetches:
        f.start()
    barrier = pltpu.get_barrier_semaphore()
    for size, stride, o in plan.peers:
        to, _ = peer_of(me, size, stride, o)
        pl.semaphore_signal(barrier, inc=1, device_id={"batch": to}, device_id_type=MESH)
    pl.semaphore_signal(barrier, inc=1, device_id=partner, device_id_type=MESH)
    pl.semaphore_wait(barrier, len(plan.peers) + 1)

    def copy(src, dst, send, recv, where):
        return pltpu.make_async_remote_copy(
            src_ref=src, dst_ref=dst, send_sem=send, recv_sem=recv, device_id=where,
            device_id_type=MESH,
        )

    pending = []
    trades = []

    def keep_out(i, src, dst):
        c = pltpu.make_async_copy(src, dst, o_sem.at[i])
        c.start()
        pending.append(c.wait)


    def trade(i, src, dst):
        c = copy(src, dst, w_send.at[i], w_recv.at[i], partner)
        c.start()
        trades.append(c)

    trade(0, tm_ref, to_ref)
    for j in range(3):
        trade(1 + j, wq_any.at[:, lanes(j * width + (1 - s) * own, own)], wqo_ref.at[:, pl.ds(j * own, own)])
    trade(4, wo_any, woo_ref)
    trade(5, wu_any, wuo_ref)
    trade(6, wd_any, wdo_ref)

    spot = lax.broadcasted_iota(jnp.int32, (1, length), 1)
    pos = jnp.where(spot < half, spot + s * half, spot - half + (1 - s) * half)
    valid = pos < len_ref[0]
    square = (slots, slots)
    eye = lax.broadcasted_iota(jnp.int32, square, 0) == lax.broadcasted_iota(jnp.int32, square, 1)
    column = jnp.sum(jnp.where(eye, gp_ref[...].astype(F32), 0.0), axis=1, keepdims=True)
    used = lax.broadcasted_iota(jnp.int32, (slots, 1), 0) < count_ref[0]
    hit = (column == pos.astype(F32)) & used
    hot = jnp.where(hit, 1.0, 0.0).astype(BF)

    def line(ref):
        return ref[...].reshape(1, ref.shape[0])

    fetches[0].wait()
    for c in trades[:4]:
        c.wait()
    bias = {0: qb_ref, 2: vb_ref}
    for j in range(3):
        w_m = wqm_ref[:, lanes(j * width + s * own, own)]
        w_o = wqo_ref[:, j * own : (j + 1) * own]
        for b, rows in enumerate((tm_ref, to_ref)):
            acc = mm(rows[:, mine], w_m) + mm(rows[:, other], w_o)
            if j in bias:
                acc = acc + bias[j][mine].reshape(1, own)
            qkv_ref[b * half : (b + 1) * half, j * own : (j + 1) * own] = acc.astype(BF)
    t_rows = (mm(hot[:, :half], tm_ref[...]) + mm(hot[:, half:], to_ref[...])).astype(BF)
    ones = jnp.ones((length, 128), BF)
    low = lax.broadcasted_iota(jnp.int32, (1, 128), 1) < HEAD_DIM
    sent = []
    for pair in range(own // 128):
        at = pair * 128
        keys = qkv_ref[:, own + at : own + at + 128]
        vals = jnp.concatenate([qkv_ref[:, 2 * own + at : 2 * own + at + 128], ones], axis=1)
        for b in (1, 0):
            q2 = qkv_ref[b * half : (b + 1) * half, at : at + 128] * jnp.array(HEAD_DIM**-0.5, BF)
            parts = []
            for e in range(2):
                q = jnp.where(low if e == 0 else ~low, q2, jnp.zeros_like(q2))
                scores = jnp.where(valid, mm_nt(q, keys), MASKED)
                top = jnp.max(scores, axis=-1, keepdims=True)
                weights = jnp.exp(scores - top).astype(BF)
                mixed = mm(weights, vals)
                parts.append(mixed[:, :128] / mixed[:, 128:])
            ctx_ref[b * half : (b + 1) * half, at : at + 128] = jnp.where(
                low, parts[0], parts[1]
            ).astype(BF)
            if b == 1:
                block = pl.ds(at, 128)
                c = copy(
                    ctx_ref.at[pl.ds(half, half), block], crecv_ref.at[pl.ds(0, half), block],
                    c_send.at[pair], c_recv.at[pair], partner,
                )
                c.start()
                sent.append(c)
    crow_ref[...] = mm(hot, ctx_ref[...]).astype(BF)
    c = copy(crow_ref, crecv_ref.at[pl.ds(half, slots)], c_send.at[3], c_recv.at[3], partner)
    c.start()
    sent.append(c)

    def place(order):
        spots, base, span = [], jnp.int32(0), n
        for size, stride in order:
            span //= size
            spots.append((base, span))
            base = base + coordinate(me, size, stride) * span
        return spots, base

    places = [place(order) for order in plan.orders]

    dims = plan.orders[0]
    levels = len(dims)
    last = levels - 1
    span = n * piece

    def window(kind, part, done, moved=None, there=None):
        spots = []
        for dim in dims:
            if dim == moved:
                spots.append(pl.ds(there, 1))
            elif dim in done:
                spots.append(pl.ds(0, dim[0]))
            else:
                spots.append(pl.ds(coordinate(me, *dim), 1))
        return gath_ref.at[(kind, s, *spots, pl.ds(*part))]

    unit = (1,) * levels
    cut = -(-slots // 32) * 16
    parts_of = [(0, cut), (cut, slots - cut)] if cut < slots else [(0, slots)]

    def gather_stage(kind, level):
        started = []
        for i, part in enumerate(parts_of):
            order = plan.orders[i % len(places)]
            dim, done = order[level], order[level + 1 :]
            size, stride = dim
            here = coordinate(me, size, stride)
            for o in range(1, size):
                to, _ = peer_of(me, size, stride, o)
                sem = (kind, i, level, o - 1)
                block = window(kind, part, done)
                src = fac_ref.at[(kind, *[pl.ds(0, 1)] * levels, pl.ds(*part))] if level == last else block
                c = copy(src, block, fa_send.at[sem], fa_recv.at[sem], {"batch": to})
                c.start()
                back = lax.rem(here + size - o, size)
                started.append((c, sem, window(kind, part, done, dim, back)))
        return started

    def gather_begin(kind, value):
        fac_ref[kind] = value.reshape(unit + value.shape)
        everything = (0, slots)
        if fused:
            here = tuple(pl.ds(coordinate(me, *dim), 1) for dim in dims)
            gath_ref[(pl.ds(kind, 1), pl.ds(s, 1), *here)] = value.reshape((1, 1) + unit + value.shape)
        else:
            keep = pltpu.make_async_copy(fac_ref.at[kind], window(kind, everything, ()), w_sem.at[4 + kind])
            keep.start()
            keep.wait()
        gathers[kind] = (last, gather_stage(kind, last))
        c = copy(fac_ref.at[kind], window(kind, everything, ()), ow_send.at[kind], ow_recv.at[kind], partner)
        c.start()
        pending.append(c.wait)

    gathers = {}

    def gather_step(kind):
        level, started = gathers[kind]
        if level < 0:
            return
        for c, _, _ in started:
            c.wait_recv()
        gathers[kind] = (level - 1, gather_stage(kind, level - 1) if level > 0 else [])
        for c, sem, theirs in started:
            f = copy(theirs, theirs, fw_send.at[sem], fw_recv.at[sem], partner)
            f.start()
            pending.append(c.wait_send)
            pending.append(f.wait)

    tracks = [place(order) for order in plan.lanes]
    depth = len(plan.lanes[0])
    bottom = depth - 1

    def reduce_start(stream, level):
        order = plan.lanes[stream % 4]
        base, span = tracks[stream % 4][0][level]
        size, stride = order[level]
        off = stream * n * piece
        ops = []
        count = sum(z - 1 for z, _ in order[:level])
        for o in range(1, size):
            to, there = peer_of(me, size, stride, o)
            src = load_ref if level == 0 else buf_ref
            at = pl.ds(pl.multiple_of(off + (base + there * span) * piece, 16), span * piece)
            slot = pl.ds(in_base(stream, level) + (o - 1) * span * piece, span * piece)
            sem = (stream, count + o - 1)
            c = copy(src.at[at], in_ref.at[slot], rs_send.at[sem], rs_recv.at[sem], {"batch": to})
            c.start()
            ops.append(c)
        return ops

    def in_base(stream, level):
        order = plan.lanes[stream % 4]
        rows, span = 0, n
        for size, _ in order[:level]:
            span //= size
            rows += (size - 1) * span
        return (stream * n + rows) * piece

    def reduce_finish(stream, level, ops):
        order = plan.lanes[stream % 4]
        base, span = tracks[stream % 4][0][level]
        size, stride = order[level]
        off = stream * n * piece
        for c in ops:
            c.wait()
        here = coordinate(me, size, stride)
        at = pl.ds(pl.multiple_of(off + (base + here * span) * piece, 16), span * piece)
        src = load_ref if level == 0 else buf_ref
        acc = src[at].astype(F32)
        for o in range(1, size):
            slot = pl.ds(in_base(stream, level) + (o - 1) * span * piece, span * piece)
            acc = acc + in_ref[slot].astype(F32)
        dst = res_ref if level == bottom else buf_ref
        dst[at] = acc.astype(BF)

    def spread_start(stream, level):
        order = plan.lanes[stream % 4]
        base, span = tracks[stream % 4][0][level]
        size, stride = order[level]
        off = stream * n * piece
        here = coordinate(me, size, stride)
        at = pl.ds(pl.multiple_of(off + (base + here * span) * piece, 16), span * piece)
        count = sum(z - 1 for z, _ in order[:level])
        ops = []
        for o in range(1, size):
            to, _ = peer_of(me, size, stride, o)
            sem = (stream, count + o - 1)
            c = copy(res_ref.at[at], res_ref.at[at], ag_send.at[sem], ag_recv.at[sem], {"batch": to})
            c.start()
            ops.append(c)
        return ops

    def small_start(level, value):
        size, stride = plan.orders[0][level]
        here = coordinate(me, size, stride)
        first = sum(z for z, _ in plan.orders[0][:level])
        sm_ref[pl.ds(first + here, 1)] = value[None]
        ops = []
        for o in range(1, size):
            to, _ = peer_of(me, size, stride, o)
            sem = first + o
            slot = pl.ds(first + here, 1)
            c = copy(sm_ref.at[slot], sm_ref.at[slot], sm_send.at[sem], sm_recv.at[sem], {"batch": to})
            c.start()
            ops.append(c)
        return ops

    def small_finish(level, ops):
        for c in ops:
            c.wait()
        size, _ = plan.orders[0][level]
        first = sum(z for z, _ in plan.orders[0][:level])
        acc = sm_ref[first]
        for o in range(1, size):
            acc = acc + sm_ref[first + o]
        return acc


    gain1, gain2 = line(g1_ref), line(g2_ref)
    fetches[1].wait()
    for c in [trades[4]] + sent:
        c.wait()
    near_c = jnp.concatenate([ctx_ref[:half], crow_ref[...]], axis=0)
    attn = mm(near_c, wom_ref[...]) + mm(crecv_ref[...], woo_ref[...]) + line(ob_ref)
    tok = jnp.concatenate([tm_ref[...], t_rows], axis=0).astype(F32)
    unit1, inv1 = norm_stats(tok + attn)
    a = unit1 * gain1 + line(s1_ref)
    ab_ref[...] = a.astype(BF)
    unit1_r, inv1_r = unit1[half:], inv1[half:]
    acc_ref[...] = a + line(db_ref)
    gather_begin(0, ab_ref[half:, mine])
    for f in fetches[2:]:
        f.wait()
    trades[5].wait()
    step = ff_own // 2
    sides = ((wdm_ref, s * ff_own), (wdo_ref, (1 - s) * ff_own))
    for part, (down, base) in enumerate(sides):
        if part == 1:
            trades[6].wait()
        for c in range(ff_own // step):
            cols = lanes(base + c * step, step)
            u = mm(ab_ref[:, mine], wum_ref[:, cols]) + mm(ab_ref[:, other], wuo_ref[:, cols])
            u = u + upb_ref[cols].reshape(1, step)
            phi = gelu_cdf(u)
            g = (u * phi).astype(BF)
            k = part * ff_own + c * step
            slope_ref[:, k : k + step] = gelu_slope(u[half:], phi[half:])
            acc_ref[...] += mm(g, down[c * step : (c + 1) * step])
    unit2, inv2 = norm_stats(acc_ref[...])
    unit2_r, inv2_r = unit2[half:], inv2[half:]
    dy = jnp.where(used, grad_ref[...].astype(F32), 0.0)
    dh2 = norm_back(dy, unit2_r, inv2_r, gain2)
    df = dh2.astype(BF)
    da_ref[...] = dh2
    gather_begin(1, pick(df, s, own))
    gather_step(0)
    out_ref[...] = (unit2[:half] * gain2 + line(s2_ref)).astype(BF)
    keep_out(0, out_ref, out_out)
    da_m = jnp.zeros((slots, own), F32)
    da_o = jnp.zeros((slots, own), F32)
    for part, (down, base) in enumerate(sides):
        for c in range(ff_own // step):
            cols = lanes(base + c * step, step)
            k = part * ff_own + c * step
            dg = mm_nt(df, down[c * step : (c + 1) * step])
            du = (dg * slope_ref[:, k : k + step]).astype(BF)
            da_m = da_m + mm_nt(du, wum_ref[:, cols])
            da_o = da_o + mm_nt(du, wuo_ref[:, cols])
    da_ref[:, mine] += da_m
    da_ref[:, other] += da_o
    da = da_ref[...]
    dh1 = norm_back(da, unit1_r, inv1_r, gain1)
    dat = dh1.astype(BF)
    d_ctx = mm_nt(dat, wom_ref[...]).astype(BF)
    gather_step(0)

    running = {}
    ready = set()

    def finished(first, end):
        ready.update(range(first, end))
        for t in range(plan.streams):
            rows = range(t * span // own, -(-min((t + 1) * span, 8 * own) // own))
            if t not in running and all(r in ready for r in rows):
                running[t] = reduce_start(t, 0)

    if load_ref.shape[0] > 8 * own:
        load_ref[8 * own :] = jnp.zeros((load_ref.shape[0] - 8 * own, own), BF)
    for h in range(2):
        g = mm_tn(crow_ref[...], dat[:, h * own : (h + 1) * own])
        load_ref[(6 + h) * own : (7 + h) * own] = g.astype(BF)
    finished(6, 8)
    scale = HEAD_DIM**-0.5
    q_rows = (mm(hot, qkv_ref[:, :own]) * scale).astype(BF)
    dq = []
    for pair in range(own // 128):
        at = pair * 128
        keys = qkv_ref[:, own + at : own + at + 128]
        vals = qkv_ref[:, 2 * own + at : 2 * own + at + 128]
        q2, c2 = q_rows[:, at : at + 128], d_ctx[:, at : at + 128]
        zero = jnp.zeros_like(q2)
        q4 = jnp.concatenate([jnp.where(low, q2, zero), jnp.where(low, zero, q2)], axis=0)
        c4 = jnp.concatenate([jnp.where(low, c2, zero), jnp.where(low, zero, c2)], axis=0)
        scores = jnp.where(valid, mm_nt(q4, keys), MASKED)
        probs = jnp.exp(scores - jnp.max(scores, axis=-1, keepdims=True))
        probs = probs / jnp.sum(probs, axis=-1, keepdims=True)
        dprobs = mm_nt(c4, vals)
        ds = probs * (dprobs - jnp.sum(probs * dprobs, axis=-1, keepdims=True))
        ds = ds.astype(BF)
        r = mm(ds, keys) * scale
        dq.append(jnp.where(low, r[:slots], r[slots:]).astype(BF))
        dp_ref[:, 3 * at : 3 * at + 128] = mm_tn(hot, dq[-1]).astype(BF)
        dp_ref[:, 3 * at + 128 : 3 * at + 256] = mm_tn(ds, q4).astype(BF)
        dp_ref[:, 3 * at + 256 : 3 * at + 384] = mm_tn(probs.astype(BF), c4).astype(BF)
        cols = slice(3 * at, 3 * at + 384)
        for side, feats in enumerate((other, mine)):
            g = mm_tn(tm_ref[:, feats], dp_ref[:half, cols]) + mm_tn(to_ref[:, feats], dp_ref[half:, cols])
            section = 2 * pair + side
            load_ref[section * own : (section + 1) * own] = g.astype(BF)
        finished(2 * pair, 2 * pair + 2)
        if pair == 0:
            gather_step(1)
    dq = jnp.concatenate(dq, axis=1)
    gather_step(0)
    gather_step(1)

    p_m = jnp.zeros((length, own), F32)
    p_o = jnp.zeros((length, own), F32)
    for pair in range(own // 128):
        for j in range(3):
            at = pair * 128
            d = dp_ref[:, 3 * at + j * 128 : 3 * at + (j + 1) * 128]
            p_m = p_m + mm_nt(d, wqm_ref[:, lanes(j * width + s * own + at, 128)])
            p_o = p_o + mm_nt(d, wqo_ref[:, j * own + at : j * own + at + 128])
    part_ref[:, mine] = p_m
    part_ref[:, other] = p_o
    dsend_ref[...] = part_ref[half:].astype(BF)
    c = copy(dsend_ref, drecv_out, d_send, d_recv, partner)
    c.start()
    pending.append(c.wait)
    high = dh1.astype(BF)
    rest = (dh1 - high.astype(F32)).astype(BF)
    near = hot[:, :half]
    dkeep_ref[...] = part_ref[:half] + mm_tn(near, high) + mm_tn(near, rest)
    keep_out(1, dkeep_ref, dkeep_out)
    total = lambda x: jnp.sum(x, axis=0, keepdims=True)
    part_ref[0:1] = total(dat.astype(F32))
    part_ref[1:2] = total(da * unit1_r)
    part_ref[2:3] = total(da)
    part_ref[3:4] = total(dy * unit2_r)
    part_ref[4:5] = total(dy)
    v_sums = [total(dp_ref[:, 384 * p + 256 : 384 * p + 384].astype(F32)) for p in range(own // 128)]
    sums = [total(dq.astype(F32)), jnp.concatenate(v_sums, axis=1)]
    sums.append(part_ref[0:5, mine])
    sums.append(jnp.zeros((1, own), F32))
    small = jnp.concatenate(sums, axis=0)

    pieces = iter(())
    if fused:
        size = 512 if ff_own % 512 == 0 else ff_own
        rows = n * slots

        def factor(kind, h):
            value = gath_ref[kind, h] if isinstance(h, int) else gath_ref[kind, pl.ds(h, 1)]
            return value.reshape(rows, own)

        def work():
            for h in range(2):
                dbias_ref[h : h + 1] = jnp.sum(factor(1, h).astype(F32), axis=0, keepdims=True)
            for c in range(ff_own // size):
                cols = lanes(s * ff_own + c * size, size)
                at = slice(c * size, (c + 1) * size)
                u = mm(factor(0, s), wum_ref[:, cols]) + mm(factor(0, 1 - s), wuo_ref[:, cols])
                u = u + upb_ref[cols].reshape(1, size)
                phi = gelu_cdf(u)
                g = (u * phi).astype(BF)
                slope = gelu_slope(u, phi)
                yield
                dg = mm_nt(factor(1, 0), wdm_ref[at, :own]) + mm_nt(factor(1, 1), wdm_ref[at, own:])
                du = (dg * slope).astype(BF)
                ubias_ref[:, at] = jnp.sum(du.astype(F32), axis=0, keepdims=True)
                yield
                for h in range(2):
                    gdn_ref[at, h * own : (h + 1) * own] = mm_tn(g, factor(1, h)).astype(BF)
                keep_out(2 + c, gdn_ref.at[at], gdn_out.at[at])
                yield
                gnear_ref[:, at] = mm_tn(factor(0, 1 - s), du).astype(BF)
                x = copy(gnear_ref.at[:, at], gfar_out.at[:, at], u_send.at[c], u_recv.at[c], partner)
                x.start()
                pending.append(x.wait)
                gup_ref[:, at] = mm_tn(factor(0, s), du).astype(BF)
                keep_out(8 + c, gup_ref.at[:, at], gup_out.at[:, at])
                yield

    def flush():
        for wait in pending:
            wait()
        pending.clear()

    cross = got_out.shape[0]
    small_ops = small_start(0, small)
    for level in range(depth):
        for t in range(plan.streams):
            if level > 0:
                next(pieces, None)
            reduce_finish(t, level, running[t])
            running[t] = reduce_start(t, level + 1) if level < bottom else spread_start(t, bottom)
        if level < levels:
            small = small_finish(level, small_ops)
            small_ops = small_start(level + 1, small) if level < last else []
        while level == 0 and gathers[1][0] >= 0:
            gather_step(1)
        if level == 0:
            flush()
            if fused:
                pieces = work()
    total_ref[...] = small
    for level in range(bottom, -1, -1):
        for t in range(plan.streams):
            next(pieces, None)
            for c in running[t]:
                c.wait()
            if level > 0:
                running[t] = spread_start(t, level - 1)
                continue
            rows_r = pl.ds(t * span, span)
            keep_out(14 + t, res_ref.at[rows_r], res_out.at[rows_r])
            for p in range(cross // own):
                if (2 * p * own + own - 1) // span == t:
                    x = copy(
                        res_ref.at[pl.ds(2 * p * own, own)], got_out.at[pl.ds(p * own, own)],
                        x_send.at[p], x_recv.at[p], partner,
                    )
                    x.start()
                    pending.append(x.wait)
    for _ in pieces:
        pass
    flush()


def ffn_kernel(
    gath_ref, wup_m, wup_o, wdn_m, upb_ref,
    gdn_ref, gup_ref, gsend_ref, bias_ref, dbias_ref,
    down_ref, near_ref, far_ref,
):
    s = lax.axis_index("seq")
    step, steps = pl.program_id(0), pl.num_programs(0)
    own = gath_ref.shape[3]
    ff_own = wdn_m.shape[0]
    size = 512 if ff_own % 512 == 0 else ff_own
    sides = pl.ds(s, 1), pl.ds(1 - s, 1)

    @pl.when(step == 0)
    def _():
        for ref in (down_ref, near_ref, far_ref, bias_ref, dbias_ref):
            ref[...] = jnp.zeros_like(ref)

    for h in range(2):
        dbias_ref[h : h + 1] += jnp.sum(gath_ref[1, h].astype(F32), axis=0, keepdims=True)
    for c in range(ff_own // size):
        cols = lanes(s * ff_own + c * size, size)
        at = slice(c * size, (c + 1) * size)
        u = mm(gath_ref[0, sides[0]][0], wup_m[:, cols])
        u = u + mm(gath_ref[0, sides[1]][0], wup_o[:, cols]) + upb_ref[:, cols]
        phi = gelu_cdf(u)
        g = (u * phi).astype(BF)
        dg = mm_nt(gath_ref[1, 0], wdn_m[at, :own]) + mm_nt(gath_ref[1, 1], wdn_m[at, own:])
        du = (dg * gelu_slope(u, phi)).astype(BF)
        bias_ref[:, at] += jnp.sum(du.astype(F32), axis=0, keepdims=True)
        for h in range(2):
            down_ref[at, h * own : (h + 1) * own] += mm_tn(g, gath_ref[1, h])
        near_ref[:, at] += mm_tn(gath_ref[0, sides[0]][0], du)
        far_ref[:, at] += mm_tn(gath_ref[0, sides[1]][0], du)

    @pl.when(step == steps - 1)
    def _():
        gsend_ref[...] = far_ref[...].astype(BF)
        gdn_ref[...] = down_ref[...].astype(BF)
        gup_ref[...] = near_ref[...].astype(BF)


def final_kernel(
    own_ref, out_ref, got_ref, gup_ref, gfar_ref, gdn_ref, dkeep_ref, drecv_ref, total_ref, ubias_ref,
    dbias_ref,
    gqkv_out, gout_out, gup_out, gdn_out, gtok_out, ub_out, db_out, *sum_outs,
):
    s = lax.axis_index("seq")
    own = got_ref.shape[2]
    width, ff_own = 2 * own, gup_ref.shape[1]
    for j in range(3):
        for p in range(own // 128):
            part = slice(j * 128, (j + 1) * 128)
            gqkv_out[:, lanes(j * width + s * own + p * 128, 128)] = own_ref[p, 1, :, part].astype(F32)
            gqkv_out[:, lanes(j * width + (1 - s) * own + p * 128, 128)] = got_ref[p, :, part].astype(F32)
    for h in range(2):
        gout_out[:, h * own : (h + 1) * own] = out_ref[h].astype(F32)
    gup_out[:, lanes(s * ff_own, ff_own)] = gup_ref[...].astype(F32)
    gup_out[:, lanes((1 - s) * ff_own, ff_own)] = gfar_ref[...].astype(F32)
    gdn_out[...] = gdn_ref[...].astype(F32)
    gtok_out[...] = (dkeep_ref[...] + drecv_ref[...].astype(F32)).astype(BF)
    ub_out[...] = ubias_ref[0]
    db_out[...] = jnp.where(s == 0, dbias_ref[0], dbias_ref[1])
    for i, ref in enumerate(sum_outs):
        ref[...] = total_ref[i]


def shape(dims, kind=BF):
    return jax.ShapeDtypeStruct(dims, kind)


def body(
    mesh, tokens, w_qkv, q_bias, v_bias, w_out, out_bias, attn_gain, attn_shift, w_up, up_bias,
    w_down, down_bias, ffn_gain, ffn_shift, seq_len, grad_pos, grad_count, out_grad,
):
    half, width = tokens.shape[1:]
    own, ff_own = w_qkv.shape[0], w_down.shape[0]
    length, slots, ff = 2 * half, grad_pos.shape[1], 2 * ff_own
    plan = Plan(mesh, 8 * own)
    n = plan.n
    dma = pltpu.SemaphoreType.DMA
    depth, widest = len(plan.orders[0]), max(size for size, _ in plan.orders[0]) - 1
    slots_small = sum(size for size, _ in plan.orders[0])
    cross, rows = 3 * own, n * slots
    fused = rows <= 1280
    sizes = tuple(size for size, _ in plan.orders[0])
    ones = (1,) * depth
    keep_ff = (lambda *dims: dims) if fused else (lambda *dims: (16, 128))
    vmem, hbm = pl.BlockSpec(memory_space=pltpu.VMEM), pl.BlockSpec(memory_space=pl.ANY)
    smem = pl.BlockSpec(memory_space=pltpu.SMEM)
    total_rows = half + slots
    extra = [shape((2, 2, *sizes, slots, own)), shape((own, ff))]
    out, res, got, total, dkeep, drecv, gdn, gup, gfar, ubias, dbias, *more = pl.pallas_call(
        functools.partial(layer_kernel, plan, fused),
        in_specs=[smem] * 2 + [vmem] * 12 + [hbm] * 4,
        out_specs=[hbm] * 3 + [vmem] + [hbm] * 5 + [vmem] * 2 + ([] if fused else [hbm, vmem]),
        out_shape=[shape((half, width)), shape((plan.rows, own)), shape((cross, own)),
                   shape((8, own), F32), shape((half, width), F32), shape((half, width)),
                   shape(keep_ff(ff_own, width)), shape(keep_ff(own, ff_own)),
                   shape(keep_ff(own, ff_own)), shape((1, ff_own), F32), shape((2, own), F32),
                   *([] if fused else extra)],
        scratch_shapes=[
            *([pltpu.VMEM(e.shape, e.dtype) for e in extra] if fused else []),
            pltpu.VMEM((half, width), BF), pltpu.VMEM((plan.rows, own), BF), pltpu.VMEM((half, width), F32),
            pltpu.VMEM(keep_ff(ff_own, width), BF), pltpu.VMEM(keep_ff(own, ff_own), BF),
            pltpu.VMEM((half, width), BF), pltpu.VMEM((own, 3 * width), BF),
            pltpu.VMEM((own, 3 * own), BF), pltpu.VMEM((own, width), BF), pltpu.VMEM((own, width), BF),
            pltpu.VMEM((own, ff), BF), pltpu.VMEM((ff_own, width), BF), pltpu.VMEM((ff_own, width), BF),
            pltpu.VMEM((length, 3 * own), BF), pltpu.VMEM((length, own), BF),
            pltpu.VMEM((slots, own), BF), pltpu.VMEM((total_rows, own), BF),
            pltpu.VMEM((total_rows, width), BF), pltpu.VMEM((total_rows, width), F32),
            pltpu.VMEM((slots, ff), F32), pltpu.VMEM((slots, width), F32),
            pltpu.VMEM((plan.rows, own), BF), pltpu.VMEM((plan.rows, own), BF),
            pltpu.VMEM((plan.rows, own), BF), pltpu.VMEM((slots_small, 8, own), F32),
            pltpu.VMEM((length, 3 * own), BF), pltpu.VMEM((length, width), F32),
            pltpu.VMEM((half, width), BF), pltpu.VMEM(keep_ff(own, ff_own), BF),
            pltpu.VMEM((2, *ones, slots, own), BF),
            dma((plan.streams, plan.copies)), dma((plan.streams, plan.copies)),
            dma((plan.streams, plan.copies)), dma((plan.streams, plan.copies)),
            dma((2, 2, depth, widest)), dma((2, 2, depth, widest)),
            dma((2, 2, depth, widest)), dma((2, 2, depth, widest)),
            dma((2,)), dma((2,)),
            dma((slots_small,)), dma((slots_small,)),
            dma((3,)), dma((3,)),
            dma, dma, dma((8,)), dma((8,)), dma((4,)), dma((4,)), dma((7,)), dma((7,)), dma((6,)), dma((14 + plan.streams,)),
        ],
        compiler_params=pltpu.CompilerParams(
            collective_id=0, has_side_effects=True, vmem_limit_bytes=VMEM_LIMIT
        ),
    )(seq_len, grad_count, tokens[0], grad_pos, out_grad[0], out_bias, attn_gain, attn_shift, down_bias,
      ffn_gain, ffn_shift, q_bias, v_bias, up_bias, w_qkv, w_out, w_up, w_down)

    if not fused:
        gath, wup_o = more
        tile = 1280 if rows % 1280 == 0 else slots
        fixed = lambda *dims: pl.BlockSpec(dims, lambda i: (0,) * len(dims), pipeline_mode=pl.Buffered(1))
        gdn, gup, gsend, ubias, dbias = pl.pallas_call(
            ffn_kernel,
            grid=(rows // tile,),
            in_specs=[pl.BlockSpec((2, 2, tile, own), lambda i: (0, 0, i, 0)), fixed(own, ff),
                      fixed(own, ff), fixed(ff_own, width), fixed(1, ff)],
            out_specs=[fixed(ff_own, width), fixed(own, ff_own), fixed(own, ff_own),
                       fixed(1, ff_own), fixed(2, own)],
            out_shape=[shape((ff_own, width)), shape((own, ff_own)), shape((own, ff_own)),
                       shape((1, ff_own), F32), shape((2, own), F32)],
            scratch_shapes=[pltpu.VMEM((ff_own, width), F32), pltpu.VMEM((own, ff_own), F32),
                            pltpu.VMEM((own, ff_own), F32)],
            compiler_params=pltpu.CompilerParams(vmem_limit_bytes=VMEM_LIMIT),
        )(gath.reshape(2, 2, rows, own), w_up, wup_o, w_down, up_bias.reshape(1, ff))
        gfar = lax.ppermute(gsend, "seq", [(0, 1), (1, 0)])
    cut = 4 if own % 64 == 0 else 1
    block = own // cut
    res = res[: 8 * own].reshape(8, own, own)
    flat = lambda r, c: pl.BlockSpec((r, c), lambda i: (i, 0))
    whole = lambda *dims: pl.BlockSpec(dims, lambda i: (0,) * len(dims))
    gqkv, gout, gup, gdn, gtok, ub, db, *sums = pl.pallas_call(
        final_kernel,
        grid=(cut,),
        in_specs=[pl.BlockSpec((3, 2, block, own), lambda i: (0, 0, i, 0)),
                  pl.BlockSpec((2, block, own), lambda i: (3, i, 0)),
                  pl.BlockSpec((3, block, own), lambda i: (0, i, 0)),
                  flat(block, ff_own), flat(block, ff_own), flat(ff_own // cut, width),
                  flat(half // cut, width), flat(half // cut, width), whole(8, own), whole(1, ff_own),
                  whole(2, own)],
        out_specs=[flat(block, 3 * width), flat(block, width), flat(block, ff),
                   flat(ff_own // cut, width), flat(half // cut, width), whole(ff_own)]
        + [whole(own)] * 8,
        out_shape=[shape((own, 3 * width), F32), shape((own, width), F32), shape((own, ff), F32),
                   shape((ff_own, width), F32), shape((half, width)), shape((ff_own,), F32)]
        + [shape((own,), F32)] * 8,
        compiler_params=pltpu.CompilerParams(vmem_limit_bytes=VMEM_LIMIT),
    )(res.reshape(4, 2, own, own), res, got.reshape(3, own, own), gup, gfar, gdn, dkeep, drecv, total, ubias, dbias)
    return (
        out[None], gtok[None], gqkv, sums[0], sums[1], gout, sums[2], sums[3], sums[4], gup, ub, gdn, db,
        sums[5], sums[6],
    )


def solution(mesh):
    specs = dict(
        in_specs=(
            P("batch", "seq", None), P("seq", None), P(), P(), P("seq", None), P(), P(), P(),
            P("seq", None), P(), P("seq", None), P(), P(), P(), P("batch"), P("batch", None),
            P("batch"), P("batch", None, None),
        ),
        out_specs=(
            P("batch", "seq", None), P("batch", "seq", None), P("seq", None), P("seq"), P("seq"),
            P("seq", None), P("seq"), P("seq"), P("seq"), P("seq", None), P("seq"),
            P("seq", None), P("seq"), P("seq"), P("seq"),
        ),
    )
    return jax.shard_map(functools.partial(body, mesh), mesh=mesh, check_vma=False, **specs)
```

time: 131 us -> 124 us (0.947)
  Pallas kernels: 114 us -> 121 us
  waiting for transfers between devices: 4.94 us -> 0 us
  local copies, waits for them, and re-layouts: 5.06 us -> 0.75 us
  other arithmetic: 2.71 us -> 0 us
  starting transfers between devices: 2.02 us -> 0 us
    pallas_call x4 -> x2, Pallas kernels: 114 us -> 121 us  [the longest x1 111 us: body(): pl.pallas_call(functools.partial(layer_kernel, plan, fused), in_specs=[sm...]
    ppermute x6 -> x0, waiting for transfers between devices: 4.94 us -> none  [body(): swap = lambda x: lax.ppermute(x, 'seq', [(0, 1), (1, 0)])]
    ppermute x6 -> x0, starting transfers between devices: 2.02 us -> none  [body(): swap = lambda x: lax.ppermute(x, 'seq', [(0, 1), (1, 0)])]
    slice x1 -> x0, local copies, waits for them, and re-layouts: 1.6 us -> none  [body(): total[6]]
    pallas_call x1 -> x0, other arithmetic: 1.31 us -> none  [body(): pl.pallas_call(functools.partial(reduce_kernel, plan, fused), in_specs=[v...]
  transfers between devices with their start and end apart: 6 -> 0, of which waited for: 2 -> 0; matrix products, arithmetic and copies ran while one was open for 3% -> 0% of each run, Pallas kernels for 5% -> 0%
where the time goes in v3:
time: 124 us; the launch traced here: 123 us
  Pallas kernels  121 us (98%)
  between operations  1.98 us (2%)
    pallas_call x1, Pallas kernels, body(): pl.pallas_call(functools.partial(layer_kernel, plan, fused), in_specs=[sm...  111 us
    pallas_call x1, Pallas kernels, body(): pl.pallas_call(final_kernel, grid=(cut,), in_specs=[pl.BlockSpec((3, 2, b...  9.41 us

profile of v3, /device:TPU:0, one launch (start us, length us, event | category | flops | bytes accessed | tf_op | source)
XLA Modules:
  0.0 123.4 jit_solution(6903039985291720325)
XLA Ops:
  1.9 111.3 %shard_map.289 = (bf16[256,768]{1,0:T(8,128)(2,1)}, bf16[3072,384]{1,0:T(8,128)(2,1)}, bf16[1152,384]{1,0:T(8,128)(2,1)}, f32[8,384]{1,0:T(8,128)}, f32[256,768]...) custom-call(s32[1]{0:T(128)S(6)} %copy.34.len_ref, ...), custom_call_target="tpu_custom_call" | custom-call | tf_op jit(solution)/shard_map/pallas_call | solution.py:738
  113.2 0.0 copy-start
  113.2 9.4 %shard_map.290 = (f32[384,2304]{1,0:T(8,128)}, f32[384,768]{1,0:T(8,128)}, f32[384,3072]{1,0:T(8,128)}, f32[1536,768]{1,0:T(8,128)}, bf16[256,768]{1,0:T(8,128)(...) custom-call(bf16[4,2,384,384]{3,2,1,0:T(8,128)(2,1)} %bitcast.7, ...), custom_call_target="tpu_custom_call" | custom-call | tf_op jit(solution)/shard_map/pallas_call | solution.py:801
  122.7 0.0 copy-done
  122.7 0.7 copy.36
Async XLA Ops:
  113.2 9.4 %copy-start = (bf16[256,768]{1,0:T(8,128)(2,1)S(1)}, bf16[256,768]{1,0:T(8,128)(2,1)}, u32[]{:S(2)}) copy-start(bf16[256,768]{1,0:T(8,128)(2,1)} %get-tuple-element.40) | copy-start | bytes 1179652
